TPU v7x, 32 devices: a whole 2x2x4 slice. The times are simulated.
32 devices in a mesh: ens: 4 (over y, core), space: 8 (over z, x).
Axes of the slice: x: 2, y: 2, z: 4, core: 2. Of those that a mesh axis runs over, the one named last changes fastest.
Arguments:
- prior_profiles: bfloat16 [128, 64, 64, 128], P('ens', 'space'), may hold values from -6 to 6
- conductivity_profile: bfloat16 [128, 64, 64, 128], P('ens', 'space'), may hold values from 0.5 to 2
- sensor_position_flat: int32 [8192], P('space'), may hold values from 0 to 65535
- observation_slot_count: int32 [8], P('space'), may hold values from 1 to 1024, 5120 in all
- obs_values: float32 [8192], P('space'), may hold values from -6 to 6
- obs_std: float32 [8192], P('space'), may hold values from 0.3 to 3
- obs_noise: float32 [128, 8192], P('ens', 'space'), may hold values from -6 to 6
- params: float32 [128, 2048], P('ens', 'space'), may hold values from -6 to 6
Outputs:
- posterior_parameters: float32 [128, 2048], P('ens', 'space')
- predicted_states: float32 [128, 64, 64, 128], P('ens', 'space')
Inputs may be any that keep to these rules, and one draw needn't show every extreme that they name: The live slots of a slab are its first observation_slot_count ones.
All inputs are finite; a program needn't handle non-finite values. No bound on the sum of `observation_slot_count` on one device may be relied on, other than what follows from the above.
Results may differ from a plain program's by a relative error of at most 0.0003.
Values may be sent and summed in bfloat16 or wider, within the bound.
A program may use at most 256 MiB of HBM per device.

v0:
```python
import functools
import math

import jax
import jax.numpy as jnp
from jax import lax
from jax.experimental import pallas as pl
from jax.experimental.pallas import tpu as pltpu
from jax.sharding import PartitionSpec as P

half_step = 0.04
HI = lax.Precision.HIGHEST
MESH = pl.DeviceIdType.MESH


def stencil_kernel(u_ref, k_ref, o_ref, t_ref):
    members, cz, nx, ny = u_ref.shape
    row = lax.broadcasted_iota(jnp.int32, (nx, ny), 0)
    lane = lax.broadcasted_iota(jnp.int32, (nx, ny), 1)
    first_x, last_x = row == 0, row == nx - 1
    first_y, last_y = lane == 0, lane == ny - 1

    def member(m, carry):
        below = None
        u = u_ref[m, 0].astype(jnp.float32)
        k = k_ref[m, 0].astype(jnp.float32)
        for z in range(cz):
            ku = k * u
            fx = (k + pltpu.roll(k, nx - 1, 0)) * (pltpu.roll(u, nx - 1, 0) - u)
            total = jnp.where(last_x, -ku, fx) - jnp.where(first_x, ku, pltpu.roll(fx, 1, 0))
            fy = (k + pltpu.roll(k, ny - 1, 1)) * (pltpu.roll(u, ny - 1, 1) - u)
            total += jnp.where(last_y, -ku, fy) - jnp.where(first_y, ku, pltpu.roll(fy, 1, 1))
            if below is not None:
                total -= below
            if z < cz - 1:
                u_next = u_ref[m, z + 1].astype(jnp.float32)
                k_next = k_ref[m, z + 1].astype(jnp.float32)
                below = (k + k_next) * (u_next - u)
                total += below
            o_ref[m, z] = u + half_step * total
            if z < cz - 1:
                u, k = u_next, k_next
        return carry

    lax.fori_loop(0, members, member, 0)

    def turn(z, carry):
        for x in range(0, nx, 8):
            tile = o_ref[:, z, x : x + 8, :]
            t_ref[pl.ds(pl.multiple_of(z * nx, nx) + x, 8)] = jnp.swapaxes(tile, 0, 1)
        return carry

    lax.fori_loop(0, cz, turn, 0)


def stencil(u, k):
    m, cz, nx, ny = u.shape
    block = 8
    spec = pl.BlockSpec((block, cz, nx, ny), lambda g: (g, 0, 0, 0))
    return pl.pallas_call(
        stencil_kernel,
        grid=(m // block,),
        in_specs=[spec, spec],
        out_specs=[spec, pl.BlockSpec((cz * nx, block, ny), lambda g: (0, g, 0))],
        out_shape=[
            jax.ShapeDtypeStruct(u.shape, jnp.float32),
            jax.ShapeDtypeStruct((cz * nx, m, ny), jnp.float32),
        ],
        cost_estimate=pl.CostEstimate(
            flops=40 * u.size, bytes_accessed=8 * u.size, transcendentals=0
        ),
        name="stencil",
    )(u, k)


def border_kernel(
    row_ref, col_ref, p_ref, u_ref, k_ref, turned_ref, ulo_ref, klo_ref, uhi_ref, khi_ref,
    o_ref, picked_ref, scr, edge, u_own, k_own, sem,
):
    cells, members, ny = scr.shape
    nx = edge.shape[2]
    cz = cells // nx
    last = cz - 1
    tile = 16

    def start(src, dst, i):
        copy = pltpu.make_async_copy(src, dst, sem.at[i])
        copy.start()
        return copy

    edges = [
        [
            start(p_ref.at[:, z], edge.at[e], 3 * e),
            start(u_ref.at[:, z], u_own.at[e], 3 * e + 1),
            start(k_ref.at[:, z], k_own.at[e], 3 * e + 2),
        ]
        for e, z in enumerate((0, last))
    ]
    inner = pl.ds(nx, cells - 2 * nx)
    load = start(turned_ref.at[inner], scr.at[inner], 6)
    stores = []
    for e, (z, un_ref, kn_ref) in enumerate(((0, ulo_ref, klo_ref), (last, uhi_ref, khi_ref))):
        for copy in edges[e]:
            copy.wait()

        def fix(t, carry):
            x = pl.multiple_of(t * tile, tile)
            for m in range(0, members, 8):
                at = (pl.ds(m, 8), pl.ds(x, tile), slice(None))
                u = u_own[(e,) + at].astype(jnp.float32)
                k = k_own[(e,) + at].astype(jnp.float32)
                un = un_ref[at].astype(jnp.float32)
                kn = kn_ref[at].astype(jnp.float32)
                new = edge[(e,) + at] + half_step * (k + kn) * (un - u)
                edge[(e,) + at] = new
                for i in range(0, tile, 8):
                    turned = jnp.swapaxes(new[:, i : i + 8, :], 0, 1)
                    scr[pl.ds(z * nx + x + i, 8), m : m + 8, :] = turned
            return carry

        lax.fori_loop(0, nx // tile, fix, 0)
        stores.append(start(edge.at[e], o_ref.at[:, z], 7 + e))
    load.wait()
    lane = lax.broadcasted_iota(jnp.int32, (members, ny), 1)
    unroll = 32

    def chunk(c, carry):
        def step(s, acc):
            for i in range(unroll):
                jj = s * unroll + i
                j = c * ny + jj
                v = pltpu.roll(scr[row_ref[j]], col_ref[j], 1)
                acc = jnp.where(lane == jj, v, acc)
            return acc

        acc = lax.fori_loop(0, ny // unroll, step, jnp.zeros((members, ny), jnp.float32))
        picked_ref[:, pl.ds(pl.multiple_of(c * ny, ny), ny)] = acc
        return carry

    lax.fori_loop(0, picked_ref.shape[1] // ny, chunk, 0)
    for copy in stores:
        copy.wait()


def border(pred, turned, u, k, ulo, klo, uhi, khi, position):
    m, cz, nx, ny = u.shape
    slots = position.shape[0]
    row = position // ny
    slot = jnp.arange(slots, dtype=jnp.int32)
    shift = (slot - position % ny) % ny
    smem = pl.BlockSpec(memory_space=pltpu.SMEM)
    vmem = pl.BlockSpec(memory_space=pltpu.VMEM)
    whole = pl.BlockSpec(memory_space=pl.ANY)
    return pl.pallas_call(
        border_kernel,
        in_specs=[smem, smem] + [whole] * 4 + [vmem] * 4,
        out_specs=[whole, vmem],
        out_shape=[
            jax.ShapeDtypeStruct(u.shape, jnp.float32),
            jax.ShapeDtypeStruct((m, slots), jnp.float32),
        ],
        scratch_shapes=[
            pltpu.VMEM(turned.shape, jnp.float32),
            pltpu.VMEM((2, m, nx, ny), jnp.float32),
            pltpu.VMEM((2, m, nx, ny), u.dtype),
            pltpu.VMEM((2, m, nx, ny), u.dtype),
            pltpu.SemaphoreType.DMA((9,)),
        ],
        input_output_aliases={2: 0},
        name="border",
    )(row, shift, pred, u, k, turned, ulo, klo, uhi, khi)


def products_kernel(
    n_e, n_s, count_ref, picked_ref, noise_ref, values_ref, std_ref, params_ref,
    gram_ref, cross_ref, all_params_ref,
    all_picked, part, parts, total,
    send_a, recv_a, send_h, recv_h, send_p, recv_p, send_s, recv_s, send_g, recv_g,
):
    own, slots = picked_ref.shape
    members = own * n_e
    me_e, me_s = lax.axis_index("ens"), lax.axis_index("space")
    scale = math.sqrt(members - 1.0)

    def ens_peer(d):
        return (lax.rem(me_e + d, n_e), me_s)

    def space_peer(d):
        return (me_e, lax.rem(me_s + d, n_s))

    barrier = pltpu.get_barrier_semaphore()
    for d in range(1, n_e):
        pl.semaphore_signal(barrier, inc=1, device_id=ens_peer(d), device_id_type=MESH)
    for d in range(1, n_s):
        pl.semaphore_signal(barrier, inc=1, device_id=space_peer(d), device_id_type=MESH)
    pl.semaphore_wait(barrier, n_e + n_s - 2)

    def send(src, dst, ssem, rsem, peer):
        copy = pltpu.make_async_remote_copy(
            src_ref=src, dst_ref=dst, send_sem=ssem, recv_sem=rsem,
            device_id=peer, device_id_type=MESH,
        )
        copy.start()
        return copy

    pair = me_e + 1 - 2 * lax.rem(me_e, 2)
    partner = (pair, me_s)
    hops = n_e // 2
    handed = [send(picked_ref, all_picked.at[me_e], send_h.at[0], recv_h.at[0], partner)]
    picked_copies = [
        send(picked_ref, all_picked.at[me_e], send_a.at[d], recv_a.at[d], ens_peer(2 * d))
        for d in range(1, hops)
    ]
    params_copies = [
        send(params_ref, all_params_ref.at[me_e], send_p.at[d], recv_p.at[d], ens_peer(d))
        for d in range(1, n_e)
    ]
    all_params_ref[me_e] = params_ref[...]
    mine = picked_ref[...]
    all_picked[me_e] = mine
    live = lax.broadcasted_iota(jnp.int32, (1, slots), 1) < count_ref[0]
    std = std_ref[...]
    inverse = jnp.where(live, 1.0 / (std * scale), 0.0)
    misfit = jnp.where(live, (values_ref[...] - mine) / std + noise_ref[...], 0.0)
    for d in range(1, hops):
        picked_copies[d - 1].wait()
        block = all_picked.at[lax.rem(me_e + n_e - 2 * d, n_e)]
        handed.append(send(block, block, send_h.at[d], recv_h.at[d], partner))
    for copy in handed:
        copy.wait()
    everyone = all_picked[...].reshape(members, slots)
    centre = jnp.sum(everyone, axis=0, keepdims=True) / members
    spread = (everyone - centre) * inverse
    left = jnp.concatenate([(mine - centre) * inverse, misfit], axis=0)
    part[...] = lax.dot_general(
        left, spread, (((1,), (1,)), ((), ())),
        precision=HI, preferred_element_type=jnp.float32,
    )
    space_copies = [
        send(part, parts.at[d], send_s.at[d], recv_s.at[d], space_peer(d)) for d in range(1, n_s)
    ]
    acc = part[...]
    for d in range(1, n_s):
        space_copies[d - 1].wait()
        acc += parts[d]
    total[...] = acc[:own]
    gram_copies = [
        send(total, gram_ref.at[me_e], send_g.at[d], recv_g.at[d], ens_peer(d))
        for d in range(1, n_e)
    ]
    gram_ref[me_e] = acc[:own]
    cross_ref[...] = acc[own:]
    for copy in gram_copies:
        copy.wait()
    for copy in params_copies:
        copy.wait()


def products(n_e, n_s, count, picked, noise, values, std, params):
    own, slots = picked.shape
    vmem = pl.BlockSpec(memory_space=pltpu.VMEM)
    dma = pltpu.SemaphoreType.DMA
    return pl.pallas_call(
        functools.partial(products_kernel, n_e, n_s),
        in_specs=[pl.BlockSpec(memory_space=pltpu.SMEM)] + [vmem] * 5,
        out_specs=[vmem] * 3,
        out_shape=[
            jax.ShapeDtypeStruct((n_e, own, n_e * own), jnp.float32),
            jax.ShapeDtypeStruct((own, n_e * own), jnp.float32),
            jax.ShapeDtypeStruct((n_e,) + params.shape, jnp.float32),
        ],
        scratch_shapes=[
            pltpu.VMEM((n_e, own, slots), jnp.float32),
            pltpu.VMEM((2 * own, n_e * own), jnp.float32),
            pltpu.VMEM((n_s, 2 * own, n_e * own), jnp.float32),
            pltpu.VMEM((own, n_e * own), jnp.float32),
        ]
        + [dma((n_e,))] * 6 + [dma((n_s,))] * 2 + [dma((n_e,))] * 2,
        compiler_params=pltpu.CompilerParams(collective_id=0, has_side_effects=True),
        name="products",
    )(count, picked, noise, values.reshape(1, -1), std.reshape(1, -1), params)


def update_kernel(gram_ref, cross_ref, all_params_ref, params_ref, o_ref, work):
    members = gram_ref.shape[1]
    own = cross_ref.shape[0]
    rows = lax.broadcasted_iota(jnp.int32, (members, members), 0)
    cols = lax.broadcasted_iota(jnp.int32, (members, members), 1)
    lane = lax.broadcasted_iota(jnp.int32, (1, members), 1)
    work[:members] = gram_ref[...] + jnp.where(rows == cols, 1.0, 0.0)
    work[members:] = cross_ref[...]

    pivots = 8
    segments = 4
    span = members // segments

    def step(lo, s, diagonal):
        first = lo + s * pivots
        t = work[lo:]
        here = [lane == first + i for i in range(pivots)]
        columns = [
            jnp.sum(jnp.where(here[i], t, 0.0), axis=1, keepdims=True) for i in range(pivots)
        ]
        rows = [work[pl.ds(first + i, 1), :] for i in range(pivots)]
        corner = [
            [jnp.sum(jnp.where(here[j], rows[i], 0.0), axis=1, keepdims=True) for j in range(pivots)]
            for i in range(pivots)
        ]
        for i in range(pivots):
            pivot = corner[i][i]
            diagonal = jnp.where(here[i], pivot, diagonal)
            inverse = 1.0 / pivot
            factor = jnp.where(here[i], 0.0, rows[i] * inverse)
            t = t - columns[i] * factor
            for j in range(i + 1, pivots):
                ratio = corner[i][j] * inverse
                columns[j] = columns[j] - columns[i] * ratio
                rows[j] = rows[j] - corner[j][i] * factor
                for l in range(i + 1, pivots):
                    corner[l][j] = corner[l][j] - corner[l][i] * ratio
        work[lo:] = t
        return diagonal

    diagonal = jnp.ones((1, members), jnp.float32)
    for part in range(segments):
        diagonal = lax.fori_loop(
            0, span // pivots, functools.partial(step, part * span), diagonal
        )
    weights = work[members:] / diagonal
    all_params = all_params_ref[...]
    centre = jnp.sum(all_params, axis=0, keepdims=True) / members
    anomaly = (all_params - centre) / math.sqrt(members - 1.0)
    o_ref[...] = params_ref[...] + jnp.dot(
        weights, anomaly, precision=HI, preferred_element_type=jnp.float32
    )


def update(gram, cross, all_params, params):
    members, own = gram.shape[2], cross.shape[0]
    return pl.pallas_call(
        update_kernel,
        out_shape=jax.ShapeDtypeStruct(params.shape, jnp.float32),
        scratch_shapes=[pltpu.VMEM((members + own, members), jnp.float32)],
        name="update",
    )(gram.reshape(members, members), cross, all_params.reshape(members, -1), params)


def shards(n_e, n_s, u, k, position, count, values, std, noise, params):
    up = [(i, i + 1) for i in range(n_s - 1)]
    down = [(i + 1, i) for i in range(n_s - 1)]
    ulo = lax.ppermute(u[:, -1], "space", up)
    klo = lax.ppermute(k[:, -1], "space", up)
    uhi = lax.ppermute(u[:, 0], "space", down)
    khi = lax.ppermute(k[:, 0], "space", down)
    pred, turned = stencil(u, k)
    pred, picked = border(pred, turned, u, k, ulo, klo, uhi, khi, position)
    gram, cross, all_params = products(n_e, n_s, count, picked, noise, values, std, params)
    return update(gram, cross, all_params, params), pred


def solution(mesh):
    in_specs = (
        P("ens", "space", None, None),
        P("ens", "space", None, None),
        P("space"),
        P("space"),
        P("space"),
        P("space"),
        P("ens", "space"),
        P("ens", "space"),
    )
    out_specs = (P("ens", "space"), P("ens", "space", None, None))
    body = functools.partial(shards, mesh.shape["ens"], mesh.shape["space"])
    return jax.shard_map(body, mesh=mesh, in_specs=in_specs, out_specs=out_specs, check_vma=False)
```

profile of v0, /device:TPU:0, one launch (start us, length us, event | category | flops | bytes accessed | tf_op | source)
XLA Modules:
  0.0 98.0 jit_solution(3079001358749432743)
XLA Ops:
  0.6 2.1 %slice_bitcast_fusion.1 = (bf16[32,64,128]{2,1,0:T(8,128)(2,1)S(1)}, bf16[32,64,128]{2,1,0:T(8,128)(2,1)}) fusion(bf16[32,8,64,128]{3,2,1,0:T(8,128)(2,1)} %u_ref.3), kind=kLoop, calls=%fused_computation.1 | loop fusion | bytes 2097152 | tf_op jit(solution)/shard_map/squeeze | solution.py:353
  2.7 4.9 %collective-permute-start = (bf16[32,64,128]{2,1,0:T(8,128)(2,1)}, bf16[32,64,128]{2,1,0:T(8,128)(2,1)S(1)}, u32[]{:S(2)}, u32[]{:S(2)}) collective-permute-start(bf16[32,64,128]{2,1,0:T(8,128)(2,1)} %get-tuple-element.19), channel_id=1, source_target_pairs={{0,1},{1,2},{2,3},{3,4},{4,5},{5,6},{6,7},{8,9},{9,10},{10,11},{11... | collective-permute-start | bytes 1572872 | tf_op jit(solution)/shard_map/ppermute | solution.py:351
  7.6 2.1 %slice_bitcast_fusion = (bf16[32,64,128]{2,1,0:T(8,128)(2,1)S(1)}, bf16[32,64,128]{2,1,0:T(8,128)(2,1)}) fusion(bf16[32,8,64,128]{3,2,1,0:T(8,128)(2,1)} %k_ref.3), kind=kLoop, calls=%fused_computation | loop fusion | bytes 2097152 | tf_op jit(solution)/shard_map/squeeze | solution.py:354
  9.7 3.4 %collective-permute-start.1 = (bf16[32,64,128]{2,1,0:T(8,128)(2,1)}, bf16[32,64,128]{2,1,0:T(8,128)(2,1)S(1)}, u32[]{:S(2)}, u32[]{:S(2)}) collective-permute-start(bf16[32,64,128]{2,1,0:T(8,128)(2,1)} %get-tuple-element.17), channel_id=1, source_target_pairs={{0,1},{1,2},{2,3},{3,4},{4,5},{5,6},{6,7},{8,9},{9,10},{10,11},{11... | collective-permute-start | bytes 1572872 | tf_op jit(solution)/shard_map/ppermute | solution.py:352
  13.2 1.3 %collective-permute-start.2 = (bf16[32,64,128]{2,1,0:T(8,128)(2,1)S(1)}, bf16[32,64,128]{2,1,0:T(8,128)(2,1)S(1)}, u32[]{:S(2)}, u32[]{:S(2)}) collective-permute-start(bf16[32,64,128]{2,1,0:T(8,128)(2,1)S(1)} %get-tuple-element.18), channel_id=1, source_target_pairs={{1,0},{2,1},{3,2},{4,3},{5,4},{6,5},{7,6},{9,8},{10,9},{11,10},{12... | collective-permute-start | bytes 1572872 | tf_op jit(solution)/shard_map/ppermute | solution.py:353
  14.5 1.3 %collective-permute-start.3 = (bf16[32,64,128]{2,1,0:T(8,128)(2,1)S(1)}, bf16[32,64,128]{2,1,0:T(8,128)(2,1)S(1)}, u32[]{:S(2)}, u32[]{:S(2)}) collective-permute-start(bf16[32,64,128]{2,1,0:T(8,128)(2,1)S(1)} %get-tuple-element.16), channel_id=1, source_target_pairs={{1,0},{2,1},{3,2},{4,3},{5,4},{6,5},{7,6},{9,8},{10,9},{11,10},{12... | collective-permute-start | bytes 1572872 | tf_op jit(solution)/shard_map/ppermute | solution.py:354
  16.4 0.0 copy-start.4
  16.4 17.9 %stencil.1 = (f32[32,8,64,128]{3,2,1,0:T(8,128)}, f32[512,32,128]{2,1,0:T(8,128)}) custom-call(bf16[32,8,64,128]{3,2,1,0:T(8,128)(2,1)} %u_ref.3, bf16[32,8,64,128]{3,2,1,0:T(8,128)(2,1)} %k_ref.3), custom_call_target="tpu_custom_call" | custom-call | flops 83886080 | bytes 16777216 | tf_op jit(solution)/shard_map/stencil/pallas_call | solution.py:60
  34.3 0.0 copy-done.4
  34.3 0.6 add_select_fusion
  34.9 7.7 %collective-permute-done.ulo_ref = bf16[32,64,128]{2,1,0:T(8,128)(2,1)S(1)} collective-permute-done((bf16[32,64,128]{2,1,0:T(8,128)(2,1)}, bf16[32,64,128]{2,1,0:T(8,128)(2,1)S(1)}, u32[]{:S(2)}, u32[]{:S(2)}) %collective-permute-start) | collective-permute-done | bytes 524320 | tf_op jit(solution)/shard_map/ppermute | solution.py:351
  42.7 0.0 copy-start
  42.7 10.1 %collective-permute-done.1.klo_ref = bf16[32,64,128]{2,1,0:T(8,128)(2,1)S(1)} collective-permute-done((bf16[32,64,128]{2,1,0:T(8,128)(2,1)}, bf16[32,64,128]{2,1,0:T(8,128)(2,1)S(1)}, u32[]{:S(2)}, u32[]{:S(2)}) %collective-permute-start.1) | collective-permute-done | bytes 524320 | tf_op jit(solution)/shard_map/ppermute | solution.py:352
  52.8 0.0 copy-start.1
  52.8 0.0 collective-permute-done.2.uhi_ref
  52.8 0.0 copy-start.2
  52.8 0.0 collective-permute-done.3.khi_ref
  52.8 0.0 copy-start.3
  52.8 0.0 copy-done
  52.8 0.8 copy-done.1
  53.6 0.1 copy-done.2
  53.8 0.2 copy-done.3
  54.0 13.6 %border.1 = (f32[32,8,64,128]{3,2,1,0:T(8,128)}, f32[32,1024]{1,0:T(8,128)}) custom-call(s32[1024]{0:T(1024)} %get-tuple-element.21.row_ref, s32[1024]{0:T(1024)} %get-tuple-element.20.col_ref, f32[32,8,64,128]{3,2,1,0:T(8,128)} %get-tuple-element.9.p_ref, bf16[32,8,64,128]{3,2,1,0:T(8,128)(2,1)} %u_ref.3, ...), custom_call_target="tpu_custom_call", output_to_operand_aliasing={{0}: (2, {})} | custom-call | tf_op jit(solution)/shard_map/border/pallas_call | solution.py:154
  67.5 22.9 %products.1 = (f32[4,32,128]{2,1,0:T(8,128)}, f32[32,128]{1,0:T(8,128)}, f32[4,32,256]{2,1,0:T(8,128)}) custom-call(s32[1]{0:T(128)S(6)} %copy.20.count_ref, f32[32,1024]{1,0:T(8,128)} %get-tuple-element.11.picked_ref, f32[32,1024]{1,0:T(8,128)} %noise_ref.1, f32[1,1024]{1,0:T(1,128)} %bitcast.22, f32[1,1024]{1,0:T(1,128)} %bitcast.23, f32[32,256]{1,0:T(8,128)} %params_ref.3), custom_call_target="tpu_custom_call" | custom-call | tf_op jit(solution)/shard_map/products/pallas_call | solution.py:263
  90.4 7.6 %update.1 = f32[32,256]{1,0:T(8,128)} custom-call(f32[128,128]{1,0:T(8,128)} %bitcast.21, f32[32,128]{1,0:T(8,128)} %get-tuple-element.13.cross_ref, f32[128,256]{1,0:T(8,128)} %bitcast.20, f32[32,256]{1,0:T(8,128)} %params_ref.3), custom_call_target="tpu_custom_call" | custom-call | tf_op jit(solution)/shard_map/update/pallas_call | solution.py:340
Async XLA Ops:
  2.7 39.9 %collective-permute-start = (bf16[32,64,128]{2,1,0:T(8,128)(2,1)}, bf16[32,64,128]{2,1,0:T(8,128)(2,1)S(1)}, u32[]{:S(2)}, u32[]{:S(2)}) collective-permute-start(bf16[32,64,128]{2,1,0:T(8,128)(2,1)} %get-tuple-element.19), channel_id=1, source_target_pairs={{0,1},{1,2},{2,3},{3,4},{4,5},{5,6},{6,7},{8,9},{9,10},{10,11},{11... | collective-permute-start | bytes 1572872 | tf_op jit(solution)/shard_map/ppermute | solution.py:351
  9.7 43.0 %collective-permute-start.1 = (bf16[32,64,128]{2,1,0:T(8,128)(2,1)}, bf16[32,64,128]{2,1,0:T(8,128)(2,1)S(1)}, u32[]{:S(2)}, u32[]{:S(2)}) collective-permute-start(bf16[32,64,128]{2,1,0:T(8,128)(2,1)} %get-tuple-element.17), channel_id=1, source_target_pairs={{0,1},{1,2},{2,3},{3,4},{4,5},{5,6},{6,7},{8,9},{9,10},{10,11},{11... | collective-permute-start | bytes 1572872 | tf_op jit(solution)/shard_map/ppermute | solution.py:352
  13.2 39.6 %collective-permute-start.2 = (bf16[32,64,128]{2,1,0:T(8,128)(2,1)S(1)}, bf16[32,64,128]{2,1,0:T(8,128)(2,1)S(1)}, u32[]{:S(2)}, u32[]{:S(2)}) collective-permute-start(bf16[32,64,128]{2,1,0:T(8,128)(2,1)S(1)} %get-tuple-element.18), channel_id=1, source_target_pairs={{1,0},{2,1},{3,2},{4,3},{5,4},{6,5},{7,6},{9,8},{10,9},{11,10},{12... | collective-permute-start | bytes 1572872 | tf_op jit(solution)/shard_map/ppermute | solution.py:353
  14.5 38.3 %collective-permute-start.3 = (bf16[32,64,128]{2,1,0:T(8,128)(2,1)S(1)}, bf16[32,64,128]{2,1,0:T(8,128)(2,1)S(1)}, u32[]{:S(2)}, u32[]{:S(2)}) collective-permute-start(bf16[32,64,128]{2,1,0:T(8,128)(2,1)S(1)} %get-tuple-element.16), channel_id=1, source_target_pairs={{1,0},{2,1},{3,2},{4,3},{5,4},{6,5},{7,6},{9,8},{10,9},{11,10},{12... | collective-permute-start | bytes 1572872 | tf_op jit(solution)/shard_map/ppermute | solution.py:354
  16.4 17.9 %copy-start.4 = (s32[1024]{0:T(1024)S(1)}, s32[1024]{0:T(1024)}, u32[]{:S(2)}) copy-start(s32[1024]{0:T(1024)} %param.10) | copy-start | bytes 12292
  42.7 10.1 %copy-start = (bf16[32,64,128]{2,1,0:T(8,128)(2,1)}, bf16[32,64,128]{2,1,0:T(8,128)(2,1)S(1)}, u32[]{:S(2)}) copy-start(bf16[32,64,128]{2,1,0:T(8,128)(2,1)S(1)} %collective-permute-done.ulo_ref) | copy-start | bytes 1572868
  52.8 0.8 copy-start.1
  52.8 1.0 copy-start.2
  52.8 1.2 %copy-start.3 = (bf16[32,64,128]{2,1,0:T(8,128)(2,1)}, bf16[32,64,128]{2,1,0:T(8,128)(2,1)S(1)}, u32[]{:S(2)}) copy-start(bf16[32,64,128]{2,1,0:T(8,128)(2,1)S(1)} %collective-permute-done.3.khi_ref) | copy-start | bytes 1572868
where the time goes:
time: 98.4 us; the launch traced here: 98 us
  Pallas kernels  61.9 us (63%)
  waiting for transfers between devices  17.8 us (18%)
  starting transfers between devices  10.9 us (11%)
  local copies, waits for them, and re-layouts  5.36 us (5%)
  between operations  1.36 us (1%)
    pallas_call x1, Pallas kernels, products(): pl.pallas_call(functools.partial(products_kernel, n_e, n_s), in_specs=[pl...  22.9 us
    pallas_call x1, Pallas kernels, stencil(): pl.pallas_call(stencil_kernel, grid=(m // block,), in_specs=[spec, spec],...  17.9 us
    pallas_call x1, Pallas kernels, border(): pl.pallas_call(border_kernel, in_specs=[smem, smem] + [whole] * 4 + [vmem...  13.6 us
    ppermute x1, waiting for transfers between devices, shards(): klo = lax.ppermute(k[:, -1], 'space', up)  10.1 us
    ppermute x1, waiting for transfers between devices, shards(): ulo = lax.ppermute(u[:, -1], 'space', up)  7.74 us
    pallas_call x1, Pallas kernels, update(): pl.pallas_call(update_kernel, out_shape=jax.ShapeDtypeStruct(params.shape...  7.63 us
    ppermute x1, starting transfers between devices, shards(): ulo = lax.ppermute(u[:, -1], 'space', up)  4.89 us
    ppermute x1, starting transfers between devices, shards(): klo = lax.ppermute(k[:, -1], 'space', up)  3.44 us
  transfers between devices with their start and end apart: 4, of which 2 were waited for; matrix products, arithmetic and copies ran while one was open for 3% of the time, Pallas kernels for 18%

commit v1 on v0

v1 whole, which is shorter than its diff:
```python
import functools
import math

import jax
import jax.numpy as jnp
from jax import lax
from jax.experimental import pallas as pl
from jax.experimental.pallas import tpu as pltpu
from jax.sharding import PartitionSpec as P

half_step = 0.04
HI = lax.Precision.HIGHEST
MESH = pl.DeviceIdType.MESH
PARTS = 4


def stencil(u_ref, k_ref, o_ref):
    members, cz, nx, ny = u_ref.shape
    row = lax.broadcasted_iota(jnp.int32, (nx, ny), 0)
    lane = lax.broadcasted_iota(jnp.int32, (nx, ny), 1)
    first_x, last_x = row == 0, row == nx - 1
    first_y, last_y = lane == 0, lane == ny - 1

    def member(m, carry):
        below = None
        u = u_ref[m, 0].astype(jnp.float32)
        k = k_ref[m, 0].astype(jnp.float32)
        for z in range(cz):
            ku = k * u
            fx = (k + pltpu.roll(k, nx - 1, 0)) * (pltpu.roll(u, nx - 1, 0) - u)
            total = jnp.where(last_x, -ku, fx) - jnp.where(first_x, ku, pltpu.roll(fx, 1, 0))
            fy = (k + pltpu.roll(k, ny - 1, 1)) * (pltpu.roll(u, ny - 1, 1) - u)
            total += jnp.where(last_y, -ku, fy) - jnp.where(first_y, ku, pltpu.roll(fy, 1, 1))
            if below is not None:
                total -= below
            if z < cz - 1:
                u_next = u_ref[m, z + 1].astype(jnp.float32)
                k_next = k_ref[m, z + 1].astype(jnp.float32)
                below = (k + k_next) * (u_next - u)
                total += below
            o_ref[m, z * nx : (z + 1) * nx] = u + half_step * total
            if z < cz - 1:
                u, k = u_next, k_next
        return carry

    lax.fori_loop(0, members, member, 0)


def solve(gram_ref, cross_ref, work):
    members = gram_ref.shape[2]
    rows = lax.broadcasted_iota(jnp.int32, (members, members), 0)
    cols = lax.broadcasted_iota(jnp.int32, (members, members), 1)
    lane = lax.broadcasted_iota(jnp.int32, (1, members), 1)
    work[:members] = gram_ref[...].reshape(members, members) + jnp.where(rows == cols, 1.0, 0.0)
    work[members:] = cross_ref[...]

    pivots = 8
    segments = 4
    span = members // segments

    def step(lo, s, diagonal):
        first = lo + s * pivots
        t = work[lo:]
        here = [lane == first + i for i in range(pivots)]
        columns = [
            jnp.sum(jnp.where(here[i], t, 0.0), axis=1, keepdims=True) for i in range(pivots)
        ]
        rows = [work[pl.ds(first + i, 1), :] for i in range(pivots)]
        corner = [
            [jnp.sum(jnp.where(here[j], rows[i], 0.0), axis=1, keepdims=True) for j in range(pivots)]
            for i in range(pivots)
        ]
        for i in range(pivots):
            pivot = corner[i][i]
            diagonal = jnp.where(here[i], pivot, diagonal)
            inverse = 1.0 / pivot
            factor = jnp.where(here[i], 0.0, rows[i] * inverse)
            t = t - columns[i] * factor
            for j in range(i + 1, pivots):
                ratio = corner[i][j] * inverse
                columns[j] = columns[j] - columns[i] * ratio
                rows[j] = rows[j] - corner[j][i] * factor
                for l in range(i + 1, pivots):
                    corner[l][j] = corner[l][j] - corner[l][i] * ratio
        work[lo:] = t
        return diagonal

    diagonal = jnp.ones((1, members), jnp.float32)
    for part in range(segments):
        diagonal = lax.fori_loop(
            0, span // pivots, functools.partial(step, part * span), diagonal
        )
    return work[members:] / diagonal


def analysis_kernel(
    n_e, n_s, pos_ref, count_ref, slots_ref, noise_ref, values_ref, std_ref, params_ref,
    u_hbm, k_hbm,
    pred_hbm, ulo_hbm, klo_hbm, uhi_hbm, khi_hbm, posterior_ref,
    u_ref, k_ref, pred, asked, answer, got, own_at, picked, all_picked, all_params,
    part, parts, total, gram, cross, work,
    load, send_q, recv_q, send_w, recv_w, send_b, recv_b,
    send_a, recv_a, send_h, recv_h, send_p, recv_p, send_s, recv_s, send_g, recv_g,
):
    own, cz, nx, ny = u_ref.shape
    slots = picked.shape[1]
    members = own * n_e
    top = cz - 1
    me_e, me_s = lax.axis_index("ens"), lax.axis_index("space")
    scale = math.sqrt(members - 1.0)
    lo_side, hi_side = me_s > 0, me_s < n_s - 1
    share = own // PARTS

    def local(src, dst, i):
        copy = pltpu.make_async_copy(src, dst, load.at[i])
        copy.start()
        return copy

    loads = [local(u_hbm, u_ref, 0), local(k_hbm, k_ref, 1)]

    def ens_peer(d):
        return (lax.rem(me_e + d, n_e), me_s)

    def space_peer(d):
        return (me_e, lax.rem(me_s + d, n_s))

    barrier = pltpu.get_barrier_semaphore()
    for d in range(1, n_e):
        pl.semaphore_signal(barrier, inc=1, device_id=ens_peer(d), device_id_type=MESH)
    for d in range(1, n_s):
        pl.semaphore_signal(barrier, inc=1, device_id=space_peer(d), device_id_type=MESH)
    pl.semaphore_wait(barrier, n_e + n_s - 2)

    def remote(src, dst, ssem, rsem, peer):
        return pltpu.make_async_remote_copy(
            src_ref=src, dst_ref=dst, send_sem=ssem, recv_sem=rsem,
            device_id=peer, device_id_type=MESH,
        )

    def send(*args):
        copy = remote(*args)
        copy.start()
        return copy

    above, under = (me_e, lax.rem(me_s + 1, n_s)), (me_e, lax.rem(me_s + n_s - 1, n_s))

    def start_pair(pair):
        for side, copies in zip((hi_side, lo_side), pair):
            @pl.when(side)
            def _():
                for copy in copies:
                    copy.start()

    def wait_recv_pair(pair):
        for side, copies in zip((lo_side, hi_side), pair):
            @pl.when(side)
            def _():
                for copy in copies:
                    copy.wait_recv()

    def wait_send_pair(pair):
        for side, copies in zip((hi_side, lo_side), pair):
            @pl.when(side)
            def _():
                for copy in copies:
                    copy.wait_send()

    ask = (
        [remote(slots_ref, asked.at[0], send_q.at[0], recv_q.at[0], above)],
        [remote(slots_ref, asked.at[1], send_q.at[1], recv_q.at[1], under)],
    )
    start_pair(ask)

    def bulk(i):
        at = pl.ds(i * share, share)
        return (
            [
                remote(u_hbm.at[at, top], ulo_hbm.at[at], send_b.at[i, 0], recv_b.at[i, 0], above),
                remote(k_hbm.at[at, top], klo_hbm.at[at], send_b.at[i, 1], recv_b.at[i, 1], above),
            ],
            [
                remote(u_hbm.at[at, 0], uhi_hbm.at[at], send_b.at[i, 2], recv_b.at[i, 2], under),
                remote(k_hbm.at[at, 0], khi_hbm.at[at], send_b.at[i, 3], recv_b.at[i, 3], under),
            ],
        )

    bulks = [bulk(i) for i in range(PARTS)]
    start_pair(bulks[0])
    params_copies = [
        send(params_ref, all_params.at[me_e], send_p.at[d], recv_p.at[d], ens_peer(d))
        for d in range(1, n_e)
    ]
    all_params[me_e] = params_ref[...]

    for copy in loads:
        copy.wait()

    wide = 256
    lane_row = lax.broadcasted_iota(jnp.int32, (ny, wide), 0)
    x_row = lax.broadcasted_iota(jnp.int32, (nx, wide), 0)
    bits_y, bits_x = int(math.log2(ny)), int(math.log2(nx))

    def coordinates(p):
        y = p & (ny - 1)
        x = lax.shift_right_logical(p, bits_y) & (nx - 1)
        return y, x, lax.shift_right_logical(p, bits_y + bits_x)

    wait_recv_pair(ask)
    for e, z in ((1, top), (0, 0)):
        def answer_chunk(c, carry):
            at = pl.ds(pl.multiple_of(c * wide, wide), wide)
            y, x, _ = coordinates(asked[e, :, at])
            hot = jnp.where(lane_row == y, 1.0, 0.0).astype(jnp.bfloat16)
            mask = (x_row == x)[None]
            for f, ref in enumerate((u_ref, k_ref)):
                layer = ref[:, z].reshape(own * nx, ny)
                g = jnp.dot(layer, hot, preferred_element_type=jnp.float32)
                g = jnp.sum(jnp.where(mask, g.reshape(own, nx, wide), 0.0), axis=1)
                answer[e, f, :, at] = g.astype(jnp.bfloat16)
            return carry

        lax.fori_loop(0, slots // wide, answer_chunk, 0)
    reply = (
        [remote(answer.at[1], got.at[0], send_w.at[0], recv_w.at[0], above)],
        [remote(answer.at[0], got.at[1], send_w.at[1], recv_w.at[1], under)],
    )
    start_pair(reply)
    for i in range(1, PARTS - 1):
        start_pair(bulks[i])

    stencil(u_ref, k_ref, pred)
    store = local(pred.at[:, pl.ds(0, cz * nx)], pred_hbm, 2)

    lane = lax.broadcasted_iota(jnp.int32, (own, ny), 1)
    rows = pred.shape[1]
    flat = pred.reshape(own * rows, ny)
    unroll = 32

    def chunk(c, carry):
        def step(s, acc):
            for i in range(unroll):
                jj = s * unroll + i
                p = pos_ref[c * ny + jj]
                at = lax.shift_right_logical(p, bits_y)
                v = flat[pl.ds(at, own, stride=rows), :]
                v = pltpu.roll(v, (jj - p) & (ny - 1), 1)
                acc = jnp.where(lane == jj, v, acc)
            return acc

        acc = lax.fori_loop(0, ny // unroll, step, jnp.zeros((own, ny), jnp.float32))
        picked[:, pl.ds(pl.multiple_of(c * ny, ny), ny)] = acc
        return carry

    lax.fori_loop(0, slots // ny, chunk, 0)

    deep_row = lax.broadcasted_iota(jnp.int32, (2 * ny, wide), 0)

    def own_chunk(c, carry):
        at = pl.ds(pl.multiple_of(c * wide, wide), wide)
        y, x, z = coordinates(slots_ref[:, at])
        spot = jnp.where(z == 0, y, jnp.where(z == top, y + ny, -1))
        hot = jnp.where(deep_row == spot, 1.0, 0.0).astype(jnp.bfloat16)
        mask = (x_row == x)[None]
        for f, ref in enumerate((u_ref, k_ref)):
            layer = jnp.concatenate([ref[:, 0], ref[:, top]], axis=2).reshape(own * nx, 2 * ny)
            g = jnp.dot(layer, hot, preferred_element_type=jnp.float32)
            own_at[f, :, at] = jnp.sum(jnp.where(mask, g.reshape(own, nx, wide), 0.0), axis=1)
        return carry

    lax.fori_loop(0, slots // wide, own_chunk, 0)

    wait_recv_pair(reply)
    _, _, z = coordinates(slots_ref[...])
    u_at, k_at = own_at[0], own_at[1]
    mine = picked[...]
    for e, here, side in ((0, z == 0, lo_side), (1, z == top, hi_side)):
        other = jnp.logical_and(here, side)
        u_n = jnp.where(other, got[e, 0].astype(jnp.float32), 0.0)
        k_n = jnp.where(other, got[e, 1].astype(jnp.float32), 0.0)
        mine = mine + jnp.where(here, half_step * (k_at + k_n) * (u_n - u_at), 0.0)
    picked[...] = mine

    pair = me_e + 1 - 2 * lax.rem(me_e, 2)
    partner = (pair, me_s)
    hops = n_e // 2
    handed = [send(picked, all_picked.at[me_e], send_h.at[0], recv_h.at[0], partner)]
    picked_copies = [
        send(picked, all_picked.at[me_e], send_a.at[d], recv_a.at[d], ens_peer(2 * d))
        for d in range(1, hops)
    ]
    all_picked[me_e] = mine
    live = lax.broadcasted_iota(jnp.int32, (1, slots), 1) < count_ref[0]
    std = std_ref[...]
    inverse = jnp.where(live, 1.0 / (std * scale), 0.0)
    misfit = jnp.where(live, (values_ref[...] - mine) / std + noise_ref[...], 0.0)
    for d in range(1, hops):
        picked_copies[d - 1].wait()
        block = all_picked.at[lax.rem(me_e + n_e - 2 * d, n_e)]
        handed.append(send(block, block, send_h.at[d], recv_h.at[d], partner))
    for copy in handed:
        copy.wait()
    everyone = all_picked[...].reshape(members, slots)
    centre = jnp.sum(everyone, axis=0, keepdims=True) / members
    spread = (everyone - centre) * inverse
    left = jnp.concatenate([(mine - centre) * inverse, misfit], axis=0)
    part[...] = lax.dot_general(
        left, spread, (((1,), (1,)), ((), ())),
        precision=HI, preferred_element_type=jnp.float32,
    )
    space_copies = [
        send(part, parts.at[d], send_s.at[d], recv_s.at[d], space_peer(d)) for d in range(1, n_s)
    ]
    start_pair(bulks[PARTS - 1])
    acc = part[...]
    for d in range(1, n_s):
        space_copies[d - 1].wait()
        acc += parts[d]
    total[...] = acc[:own]
    gram_copies = [
        send(total, gram.at[me_e], send_g.at[d], recv_g.at[d], ens_peer(d))
        for d in range(1, n_e)
    ]
    gram[me_e] = acc[:own]
    cross[...] = acc[own:]
    for copy in gram_copies:
        copy.wait()
    for copy in params_copies:
        copy.wait()
    weights = solve(gram, cross, work)
    everyones = all_params[...].reshape(members, -1)
    centre = jnp.sum(everyones, axis=0, keepdims=True) / members
    anomaly = (everyones - centre) / math.sqrt(members - 1.0)
    posterior_ref[...] = params_ref[...] + jnp.dot(
        weights, anomaly, precision=HI, preferred_element_type=jnp.float32
    )

    store.wait()
    for pair in bulks:
        wait_recv_pair(pair)
    for pair in [ask, reply] + bulks:
        wait_send_pair(pair)


def analysis(n_e, n_s, position, count, noise, values, std, params, u, k):
    own, cz, nx, ny = u.shape
    slots = position.shape[0]
    members = own * n_e
    vmem = pl.BlockSpec(memory_space=pltpu.VMEM)
    smem = pl.BlockSpec(memory_space=pltpu.SMEM)
    whole = pl.BlockSpec(memory_space=pl.ANY)
    dma = pltpu.SemaphoreType.DMA
    f32 = jnp.float32
    layer = jax.ShapeDtypeStruct((own, nx, ny), u.dtype)
    return pl.pallas_call(
        functools.partial(analysis_kernel, n_e, n_s),
        in_specs=[smem, smem] + [vmem] * 5 + [whole] * 2,
        out_specs=[whole] * 5 + [vmem],
        out_shape=[jax.ShapeDtypeStruct((own, cz * nx, ny), f32)]
        + [layer] * 4
        + [jax.ShapeDtypeStruct(params.shape, f32)],
        scratch_shapes=[
            pltpu.VMEM(u.shape, u.dtype),
            pltpu.VMEM(k.shape, k.dtype),
            pltpu.VMEM((own, cz * nx + 8, ny), f32),
            pltpu.VMEM((2, 1, slots), jnp.int32),
            pltpu.VMEM((2, 2, own, slots), u.dtype),
            pltpu.VMEM((2, 2, own, slots), u.dtype),
            pltpu.VMEM((2, own, slots), f32),
            pltpu.VMEM((own, slots), f32),
            pltpu.VMEM((n_e, own, slots), f32),
            pltpu.VMEM((n_e,) + params.shape, f32),
            pltpu.VMEM((2 * own, members), f32),
            pltpu.VMEM((n_s, 2 * own, members), f32),
            pltpu.VMEM((own, members), f32),
            pltpu.VMEM((n_e, own, members), f32),
            pltpu.VMEM((own, members), f32),
            pltpu.VMEM((members + own, members), f32),
            dma((3,)),
        ]
        + [dma((2,))] * 4
        + [dma((PARTS, 4))] * 2
        + [dma((n_e,))] * 6
        + [dma((n_s,))] * 2
        + [dma((n_e,))] * 2,
        compiler_params=pltpu.CompilerParams(collective_id=0, has_side_effects=True),
        name="analysis",
    )(
        position, count, position.reshape(1, -1), noise, values.reshape(1, -1),
        std.reshape(1, -1), params, u, k,
    )


def finish_kernel(
    n_s, pred_ref, ub_ref, kb_ref, ut_ref, kt_ref, ulo_ref, klo_ref, uhi_ref, khi_ref, post_ref,
    o_ref, posterior_ref,
):
    block, cells, ny = pred_ref.shape
    cz, nx = o_ref.shape[1:3]
    me = lax.axis_index("space")
    f32 = jnp.float32
    posterior_ref[...] = post_ref[...]
    for m in range(block):
        for z in range(cz):
            new = pred_ref[m, z * nx : (z + 1) * nx]
            for e, u_ref, k_ref, un_ref, kn_ref, side in (
                (0, ub_ref, kb_ref, ulo_ref, klo_ref, me > 0),
                (cz - 1, ut_ref, kt_ref, uhi_ref, khi_ref, me < n_s - 1),
            ):
                if z == e:
                    un = jnp.where(side, un_ref[m].astype(f32), 0.0)
                    kn = jnp.where(side, kn_ref[m].astype(f32), 0.0)
                    u, k = u_ref[m, 0].astype(f32), k_ref[m, 0].astype(f32)
                    new = new + half_step * (k + kn) * (un - u)
            o_ref[m, z] = new


def finish(n_s, pred, u, k, ulo, klo, uhi, khi, posterior):
    m, cz, nx, ny = u.shape
    block = 4
    low = pl.BlockSpec((block, 1, nx, ny), lambda g: (g, 0, 0, 0))
    high = pl.BlockSpec((block, 1, nx, ny), lambda g: (g, cz - 1, 0, 0))
    halo = pl.BlockSpec((block, nx, ny), lambda g: (g, 0, 0))
    small = pl.BlockSpec(posterior.shape, lambda g: (0, 0))
    return pl.pallas_call(
        functools.partial(finish_kernel, n_s),
        grid=(m // block,),
        in_specs=[pl.BlockSpec((block, cz * nx, ny), lambda g: (g, 0, 0)), low, low, high, high]
        + [halo] * 4
        + [small],
        out_specs=[pl.BlockSpec((block, cz, nx, ny), lambda g: (g, 0, 0, 0)), small],
        out_shape=[
            jax.ShapeDtypeStruct(u.shape, jnp.float32),
            jax.ShapeDtypeStruct(posterior.shape, jnp.float32),
        ],
        name="finish",
    )(pred, u, k, u, k, ulo, klo, uhi, khi, posterior)


def shards(n_e, n_s, u, k, position, count, values, std, noise, params):
    *fields, posterior = analysis(n_e, n_s, position, count, noise, values, std, params, u, k)
    pred, ulo, klo, uhi, khi = fields
    pred, posterior = finish(n_s, pred, u, k, ulo, klo, uhi, khi, posterior)
    return posterior, pred


def solution(mesh):
    in_specs = (
        P("ens", "space", None, None),
        P("ens", "space", None, None),
        P("space"),
        P("space"),
        P("space"),
        P("space"),
        P("ens", "space"),
        P("ens", "space"),
    )
    out_specs = (P("ens", "space"), P("ens", "space", None, None))
    body = functools.partial(shards, mesh.shape["ens"], mesh.shape["space"])
    return jax.shard_map(body, mesh=mesh, in_specs=in_specs, out_specs=out_specs, check_vma=False)
```

time: 98.4 us -> 75.8 us (0.77)
  waiting for transfers between devices: 17.8 us -> 0 us
  Pallas kernels: 61.9 us -> 74.1 us
  starting transfers between devices: 10.9 us -> 0 us
  local copies, waits for them, and re-layouts: 5.36 us -> 0 us
    ppermute x4 -> x0, waiting for transfers between devices: 17.8 us -> none  [the longest x1 10.1 us: shards(): klo = lax.ppermute(k[:, -1], 'space', up)]
    pallas_call x4 -> x2, Pallas kernels: 61.9 us -> 74.1 us  [the longest x1 64.5 us: analysis(): pl.pallas_call(functools.partial(analysis_kernel, n_e, n_s), in_specs=[sm...]
    ppermute x4 -> x0, starting transfers between devices: 10.9 us -> none  [the longest x1 4.89 us: shards(): ulo = lax.ppermute(u[:, -1], 'space', up)]
    squeeze x2 -> x0, local copies, waits for them, and re-layouts: 4.21 us -> none  [the longest x1 2.11 us: shards(): khi = lax.ppermute(k[:, 0], 'space', down)]
    unnamed x10 -> x0, local copies, waits for them, and re-layouts: 1.15 us -> none
  transfers between devices with their start and end apart: 4 -> 0, of which waited for: 2 -> 0; matrix products, arithmetic and copies ran while one was open for 3% -> 0% of each run, Pallas kernels for 18% -> 0%
where the time goes in v1:
time: 75.8 us; the launch traced here: 75.4 us
  Pallas kernels  74.1 us (98%)
  between operations  1.28 us (2%)
    pallas_call x1, Pallas kernels, analysis(): pl.pallas_call(functools.partial(analysis_kernel, n_e, n_s), in_specs=[sm...  64.5 us
    pallas_call x1, Pallas kernels, finish(): pl.pallas_call(functools.partial(finish_kernel, n_s), grid=(m // block,),...  9.62 us

profile of v1, /device:TPU:0, one launch (start us, length us, event | category | flops | bytes accessed | tf_op | source)
XLA Modules:
  0.0 75.4 jit_solution(4950189402627604857)
XLA Ops:
  1.3 64.5 %analysis.1 = (f32[32,512,128]{2,1,0:T(8,128)}, bf16[32,64,128]{2,1,0:T(8,128)(2,1)}, bf16[32,64,128]{2,1,0:T(8,128)(2,1)}, bf16[32,64,128]{2,1,0:T(8,128)(2,1)}...) custom-call(s32[1024]{0:T(1024)} %pos_ref.1, s32[1]{0:T(128)S(6)} %copy.10.count_ref, s32[1,1024]{1,0:T(1,128)} %bitcast.3, ...), custom_call_target="tpu_custom_call" | custom-call | tf_op jit(solution)/shard_map/analysis/pallas_call | solution.py:354
  65.8 9.6 %finish.1 = (f32[32,8,64,128]{3,2,1,0:T(8,128)}, f32[32,256]{1,0:T(8,128)}) custom-call(f32[32,512,128]{2,1,0:T(8,128)} %get-tuple-element.10.pred_ref, bf16[32,8,64,128]{3,2,1,0:T(8,128)(2,1)} %ut_ref.1, bf16[32,8,64,128]{3,2,1,0:T(8,128)(2,1)} %kt_ref.1, bf16[32,8,64,128]{3,2,1,0:T(8,128)(2,1)} %ut_ref.1, bf16[32,8,64,128]{3,2,1,0:T(8,128)(2,1)} %kt_ref.1, ...), custom_call_target="tpu_custom_call" | custom-call | tf_op jit(solution)/shard_map/finish/pallas_call | solution.py:424

commit v2 on v1

v2 whole, which is shorter than its diff:
```python
import functools
import math

import jax
import jax.numpy as jnp
from jax import lax
from jax.experimental import pallas as pl
from jax.experimental.pallas import tpu as pltpu
from jax.sharding import PartitionSpec as P

half_step = 0.04
HI = lax.Precision.HIGHEST
MESH = pl.DeviceIdType.MESH
VMEM_BYTES = 67043328
PARTS = 4
PAD = 8
WIDE = 256
f32 = jnp.float32
bf16 = jnp.bfloat16


def pad_rows(fu, fk):
    nx = fu.shape[2] - 2 * PAD
    for f in (fu, fk):
        zero = jnp.zeros(f.shape[:2] + (PAD, f.shape[3]), f32)
        f[:, :, :PAD] = zero
        f[:, :, PAD + nx :] = zero


def stencil(lo, hi, u_ref, k_ref, o_ref, fu, fk, fy):
    cz, nx, ny = u_ref.shape[1:]
    group = fu.shape[0]
    r = lax.broadcasted_iota(jnp.int32, (ny, ny), 0)
    c = lax.broadcasted_iota(jnp.int32, (ny, ny), 1)
    eye, following, previous = r == c, r == c + 1, r + 1 == c
    one = lambda mask: jnp.where(mask, 1.0, 0.0)
    plus = [one(following) + one(eye), one(previous) + one(eye)]
    minus = [one(following) - one(eye), one(previous) - one(eye)]
    plus = jnp.concatenate(plus, axis=1).astype(bf16)
    minus = jnp.concatenate(minus, axis=1).astype(bf16)
    span = 32

    def members(i, carry):
        first = lo + i * group
        for w in range(group):
            ks = k_ref[first + w].reshape(cz * nx, ny)
            us = u_ref[first + w].reshape(cz * nx, ny)
            flux = jnp.dot(ks, plus, preferred_element_type=f32) * jnp.dot(
                us, minus, preferred_element_type=f32
            )
            fy[w] = flux[:, :ny] + flux[:, ny:]
            for z in range(cz):
                fu[w, z, PAD : PAD + nx] = u_ref[first + w, z].astype(f32)
                fk[w, z, PAD : PAD + nx] = k_ref[first + w, z].astype(f32)
        for w in range(group):
            for x in range(0, nx, span):
                at = slice(PAD + x, PAD + x + span)
                after = slice(PAD + x + 1, PAD + x + span + 1)
                before = slice(PAD + x - 1, PAD + x + span - 1)
                below = None
                u, k = fu[w, 0, at], fk[w, 0, at]
                for z in range(cz):
                    total = (k + fk[w, z, after]) * (fu[w, z, after] - u)
                    total += (k + fk[w, z, before]) * (fu[w, z, before] - u)
                    total += fy[w, z * nx + x : z * nx + x + span]
                    if below is not None:
                        total -= below
                    if z < cz - 1:
                        u_next, k_next = fu[w, z + 1, at], fk[w, z + 1, at]
                        below = (k + k_next) * (u_next - u)
                        total += below
                    o_ref[first + w, z * nx + x : z * nx + x + span] = u + half_step * total
                    if z < cz - 1:
                        u, k = u_next, k_next
        return carry

    lax.fori_loop(0, (hi - lo) // group, members, 0)


def solve(gram_ref, cross_ref, work):
    members = gram_ref.shape[2]
    rows = lax.broadcasted_iota(jnp.int32, (members, members), 0)
    cols = lax.broadcasted_iota(jnp.int32, (members, members), 1)
    lane = lax.broadcasted_iota(jnp.int32, (1, members), 1)
    work[:members] = gram_ref[...].reshape(members, members) + jnp.where(rows == cols, 1.0, 0.0)
    work[members:] = cross_ref[...]

    pivots = 8
    segments = 4
    span = members // segments

    def step(lo, s, diagonal):
        first = lo + s * pivots
        t = work[lo:]
        here = [lane == first + i for i in range(pivots)]
        columns = [
            jnp.sum(jnp.where(here[i], t, 0.0), axis=1, keepdims=True) for i in range(pivots)
        ]
        rows = [work[pl.ds(first + i, 1), :] for i in range(pivots)]
        corner = [
            [jnp.sum(jnp.where(here[j], rows[i], 0.0), axis=1, keepdims=True) for j in range(pivots)]
            for i in range(pivots)
        ]
        for i in range(pivots):
            pivot = corner[i][i]
            diagonal = jnp.where(here[i], pivot, diagonal)
            inverse = 1.0 / pivot
            factor = jnp.where(here[i], 0.0, rows[i] * inverse)
            t = t - columns[i] * factor
            for j in range(i + 1, pivots):
                ratio = corner[i][j] * inverse
                columns[j] = columns[j] - columns[i] * ratio
                rows[j] = rows[j] - corner[j][i] * factor
                for l in range(i + 1, pivots):
                    corner[l][j] = corner[l][j] - corner[l][i] * ratio
        work[lo:] = t
        return diagonal

    diagonal = jnp.ones((1, members), jnp.float32)
    for part in range(segments):
        diagonal = lax.fori_loop(
            0, span // pivots, functools.partial(step, part * span), diagonal
        )
    return work[members:] / diagonal


def analysis_kernel(
    n_e, n_s, pos_ref, count_ref, slots_hbm, noise_hbm, values_hbm, std_hbm, params_hbm,
    u_hbm, k_hbm,
    pred, posterior_ref,
    u_ref, k_ref, fu, fk, fy, ulo, klo, uhi, khi, flux, back, ret,
    slots_ref, noise_ref, values_ref, std_ref, asked, answer, got, picked, all_picked,
    all_params, part, parts, total, gram, cross, work,
    load, send_q, recv_q, send_w, recv_w, send_b, recv_b, send_r, recv_r,
    send_a, recv_a, send_h, recv_h, send_p, recv_p, send_s, recv_s, send_g, recv_g,
):
    own, cz, nx, ny = u_ref.shape
    slots = slots_ref.shape[1]
    chunks = slots // WIDE
    members = own * n_e
    half = own // 2
    share = half // PARTS
    top = cz - 1
    me_e, me_s = lax.axis_index("ens"), lax.axis_index("space")
    scale = math.sqrt(members - 1.0)
    lo_side, hi_side = me_s > 0, me_s < n_s - 1

    def local(src, dst, i):
        copy = pltpu.make_async_copy(src, dst, load.at[i])
        copy.start()
        return copy

    first, second = pl.ds(0, half), pl.ds(half, half)
    loads = [
        local(u_hbm.at[first], u_ref.at[first], 0),
        local(k_hbm.at[first], k_ref.at[first], 1),
        local(u_hbm.at[second], u_ref.at[second], 2),
        local(k_hbm.at[second], k_ref.at[second], 3),
    ]
    small = [
        local(slots_hbm, slots_ref, 4),
        local(noise_hbm, noise_ref, 5),
        local(values_hbm, values_ref, 6),
        local(std_hbm, std_ref, 7),
        local(params_hbm, all_params.at[me_e], 8),
    ]

    def ens_peer(d):
        return (lax.rem(me_e + d, n_e), me_s)

    def space_peer(d):
        return (me_e, lax.rem(me_s + d, n_s))

    barrier = pltpu.get_barrier_semaphore()
    for d in range(1, n_e):
        pl.semaphore_signal(barrier, inc=1, device_id=ens_peer(d), device_id_type=MESH)
    for d in range(1, n_s):
        pl.semaphore_signal(barrier, inc=1, device_id=space_peer(d), device_id_type=MESH)
    pad_rows(fu, fk)
    pl.semaphore_wait(barrier, n_e + n_s - 2)

    def remote(src, dst, ssem, rsem, peer):
        return pltpu.make_async_remote_copy(
            src_ref=src, dst_ref=dst, send_sem=ssem, recv_sem=rsem,
            device_id=peer, device_id_type=MESH,
        )

    def send(*args):
        copy = remote(*args)
        copy.start()
        return copy

    above, under = (me_e, lax.rem(me_s + 1, n_s)), (me_e, lax.rem(me_s + n_s - 1, n_s))

    def on_sides(sides, pair, what):
        for side, copies in zip(sides, pair):
            @pl.when(side)
            def _():
                for copy in copies:
                    getattr(copy, what)()

    def start_pair(pair):
        on_sides((hi_side, lo_side), pair, "start")

    def wait_send_pair(pair):
        on_sides((hi_side, lo_side), pair, "wait_send")

    def wait_recv_pair(pair):
        on_sides((lo_side, hi_side), pair, "wait_recv")

    ask = (
        [remote(slots_hbm, asked.at[0], send_q.at[0], recv_q.at[0], above)],
        [remote(slots_hbm, asked.at[1], send_q.at[1], recv_q.at[1], under)],
    )
    start_pair(ask)

    def bulk(i):
        at, src_up, src_down = (
            pl.ds(i * share, share), pl.ds(i * share, share), pl.ds(half + i * share, share)
        )
        s, r = send_b.at[i], recv_b.at[i]
        return (
            [
                remote(u_hbm.at[src_up, top], ulo.at[at], s.at[0], r.at[0], above),
                remote(k_hbm.at[src_up, top], klo.at[at], s.at[1], r.at[1], above),
            ],
            [
                remote(u_hbm.at[src_down, 0], uhi.at[at], s.at[2], r.at[2], under),
                remote(k_hbm.at[src_down, 0], khi.at[at], s.at[3], r.at[3], under),
            ],
        )

    def returned(i):
        at = pl.ds(i * share, share)
        s, r = send_r.at[i], recv_r.at[i]
        return (
            [remote(back.at[1, at], ret.at[0, at], s.at[0], r.at[0], above)],
            [remote(back.at[0, at], ret.at[1, at], s.at[1], r.at[1], under)],
        )

    bulks = [bulk(i) for i in range(PARTS)]
    returns = [returned(i) for i in range(PARTS)]

    def border(i):
        wait_recv_pair(bulks[i])

        def one(m, carry):
            for e, z, shift, un_ref, kn_ref, side in (
                (0, 0, 0, ulo, klo, lo_side), (1, top, half, uhi, khi, hi_side),
            ):
                un = jnp.where(side, un_ref[m].astype(f32), 0.0)
                kn = jnp.where(side, kn_ref[m].astype(f32), 0.0)
                u, k = u_ref[m + shift, z].astype(f32), k_ref[m + shift, z].astype(f32)
                value = half_step * (k + kn) * (un - u)
                flux[e, m] = value
                back[e, m] = value.astype(bf16)
            return carry

        lax.fori_loop(i * share, (i + 1) * share, one, 0)
        start_pair(returns[i])

    start_pair(bulks[0])
    start_pair(bulks[1])
    params_copies = [
        send(params_hbm, all_params.at[me_e], send_p.at[d], recv_p.at[d], ens_peer(d))
        for d in range(1, n_e)
    ]

    for copy in loads[:2]:
        copy.wait()
    stencil(0, half, u_ref, k_ref, pred, fu, fk, fy)
    for copy in loads[2:] + small:
        copy.wait()

    lane_row = lax.broadcasted_iota(jnp.int32, (ny, WIDE), 0)
    deep_row = lax.broadcasted_iota(jnp.int32, (2 * ny, WIDE), 0)
    x_row = lax.broadcasted_iota(jnp.int32, (nx, WIDE), 0)
    bits_y, bits_x = int(math.log2(ny)), int(math.log2(nx))

    def coordinates(p):
        y = p & (ny - 1)
        x = lax.shift_right_logical(p, bits_y) & (nx - 1)
        return y, x, lax.shift_right_logical(p, bits_y + bits_x)

    def columns(c):
        return pl.ds(pl.multiple_of(c * WIDE, WIDE), WIDE)

    def pick(layer, hot, mask):
        g = jnp.dot(layer, hot, preferred_element_type=f32)
        return jnp.sum(jnp.where(mask, g.reshape(own, nx, WIDE), 0.0), axis=1)

    wait_recv_pair(ask)
    for e, z in ((1, top), (0, 0)):
        def answer_chunk(c, carry):
            at = columns(c)
            y, x, _ = coordinates(asked[e, :, at])
            hot = jnp.where(lane_row == y, 1.0, 0.0).astype(bf16)
            mask = (x_row == x)[None]
            for f, ref in enumerate((u_ref, k_ref)):
                layer = ref[:, z].reshape(own * nx, ny)
                answer[e, f, :, at] = pick(layer, hot, mask).astype(bf16)
            return carry

        lax.fori_loop(0, chunks, answer_chunk, 0)
    reply = (
        [remote(answer.at[1], got.at[0], send_w.at[0], recv_w.at[0], above)],
        [remote(answer.at[0], got.at[1], send_w.at[1], recv_w.at[1], under)],
    )
    start_pair(reply)
    for i in range(2, PARTS):
        start_pair(bulks[i])
    border(0)
    border(1)
    stencil(half, own, u_ref, k_ref, pred, fu, fk, fy)
    wait_recv_pair(reply)

    lane = lax.broadcasted_iota(jnp.int32, (own, ny), 1)
    rows = pred.shape[1]
    flat = pred.reshape(own * rows, ny)
    pair = me_e + 1 - 2 * lax.rem(me_e, 2)
    partner = (pair, me_s)
    hops = n_e // 2

    def hand(d, c):
        block = all_picked.at[lax.rem(me_e + n_e - 2 * d, n_e), c]
        src = picked.at[c] if d == 0 else block
        return remote(src, block, send_h.at[d, c], recv_h.at[d, c], partner)

    def across(d, c):
        dst = all_picked.at[me_e, c]
        return remote(picked.at[c], dst, send_a.at[d, c], recv_a.at[d, c], ens_peer(2 * d))

    def relay(c):
        for d in range(1, hops):
            across(d, c).wait_recv()
            hand(d, c).start()

    def reading(c, carry):
        at = columns(c)
        y, x, z = coordinates(slots_ref[:, at])
        spot = jnp.where(z == 0, y, jnp.where(z == top, y + ny, -1))
        hot = jnp.where(deep_row == spot, 1.0, 0.0).astype(bf16)
        mask = (x_row == x)[None]
        u_at, k_at = (
            pick(
                jnp.concatenate([ref[:, 0], ref[:, top]], axis=2).reshape(own * nx, 2 * ny),
                hot, mask,
            )
            for ref in (u_ref, k_ref)
        )
        change = jnp.zeros((own, WIDE), f32)
        for e, here, side in ((0, z == 0, lo_side), (1, z == top, hi_side)):
            other = jnp.logical_and(here, side)
            u_n = jnp.where(other, got[e, 0, :, at].astype(f32), 0.0)
            k_n = jnp.where(other, got[e, 1, :, at].astype(f32), 0.0)
            change += jnp.where(here, half_step * (k_at + k_n) * (u_n - u_at), 0.0)
        for h in range(0, WIDE, ny):
            def step(s, acc):
                for i in range(unroll):
                    jj = s * unroll + i
                    p = pos_ref[c * WIDE + h + jj]
                    v = flat[pl.ds(lax.shift_right_logical(p, bits_y), own, stride=rows), :]
                    v = pltpu.roll(v, (jj - p) & (ny - 1), 1)
                    acc = jnp.where(lane == jj, v, acc)
                return acc

            unroll = ny // 2
            acc = lax.fori_loop(0, ny // unroll, step, jnp.zeros((own, ny), f32))
            picked[c, :, h : h + ny] = acc + change[:, h : h + ny]
        all_picked[me_e, c] = picked[c]
        hand(0, c).start()
        for d in range(1, hops):
            across(d, c).start()

        @pl.when(c > 0)
        def _():
            relay(c - 1)

        return carry

    lax.fori_loop(0, chunks, reading, 0)
    border(2)
    relay(chunks - 1)

    part[...] = jnp.zeros_like(part)

    def product(c, carry):
        at = columns(c)
        for d in range(hops):
            hand(d, c).wait_recv()
        mine = picked[c]
        live = lax.broadcasted_iota(jnp.int32, (1, WIDE), 1) + c * WIDE < count_ref[0]
        std = std_ref[:, at]
        inverse = jnp.where(live, 1.0 / (std * scale), 0.0)
        misfit = jnp.where(live, (values_ref[:, at] - mine) / std + noise_ref[:, at], 0.0)
        everyone = all_picked[:, c].reshape(members, WIDE)
        centre = jnp.sum(everyone, axis=0, keepdims=True) / members
        spread = (everyone - centre) * inverse
        left = jnp.concatenate([(mine - centre) * inverse, misfit], axis=0)
        part[...] += lax.dot_general(
            left, spread, (((1,), (1,)), ((), ())),
            precision=HI, preferred_element_type=f32,
        )
        return carry

    lax.fori_loop(0, chunks, product, 0)
    space_copies = [
        send(part, parts.at[d], send_s.at[d], recv_s.at[d], space_peer(d)) for d in range(1, n_s)
    ]
    for i in range(3, PARTS):
        border(i)
    acc = part[...]
    for d in range(1, n_s):
        space_copies[d - 1].wait()
        acc += parts[d]
    total[...] = acc[:own]
    gram_copies = [
        send(total, gram.at[me_e], send_g.at[d], recv_g.at[d], ens_peer(d))
        for d in range(1, n_e)
    ]
    gram[me_e] = acc[:own]
    cross[...] = acc[own:]

    def add_flux(m, carry):
        bottom, upper = pl.ds(0, nx), pl.ds(top * nx, nx)
        pred[m, bottom] = pred[m, bottom] + flux[0, m]
        pred[m + half, upper] = pred[m + half, upper] + flux[1, m]
        return carry

    lax.fori_loop(0, half, add_flux, 0)
    for copy in gram_copies:
        copy.wait()
    for copy in params_copies:
        copy.wait()
    weights = solve(gram, cross, work)
    everyones = all_params[...].reshape(members, -1)
    centre = jnp.sum(everyones, axis=0, keepdims=True) / members
    anomaly = (everyones - centre) / math.sqrt(members - 1.0)
    posterior_ref[...] = all_params[me_e] + jnp.dot(
        weights, anomaly, precision=HI, preferred_element_type=f32
    )

    def add_returned(m, carry):
        for e, z, shift, side in ((0, 0, half, lo_side), (1, top, 0, hi_side)):
            at = pl.ds(z * nx, nx)
            u, k = u_ref[m + shift, z].astype(f32), k_ref[m + shift, z].astype(f32)
            lost = jnp.where(side, ret[e, m].astype(f32), half_step * k * u)
            pred[m + shift, at] = pred[m + shift, at] - lost
        return carry

    for i in range(PARTS):
        wait_recv_pair(returns[i])
        lax.fori_loop(i * share, (i + 1) * share, add_returned, 0)

    for pair in [ask, reply] + bulks + returns:
        wait_send_pair(pair)

    def drain(c, carry):
        for d in range(hops):
            hand(d, c).wait_send()
        for d in range(1, hops):
            across(d, c).wait_send()
        return carry

    lax.fori_loop(0, chunks, drain, 0)


def analysis(n_e, n_s, position, count, noise, values, std, params, u, k):
    own, cz, nx, ny = u.shape
    slots = position.shape[0]
    chunks = slots // WIDE
    members = own * n_e
    half = own // 2
    vmem = pl.BlockSpec(memory_space=pltpu.VMEM)
    smem = pl.BlockSpec(memory_space=pltpu.SMEM)
    hbm = pl.BlockSpec(memory_space=pltpu.HBM)
    dma = pltpu.SemaphoreType.DMA
    field = (own, cz * nx + PAD, ny)
    layers = pltpu.VMEM((half, nx, ny), u.dtype)
    group = 4
    return pl.pallas_call(
        functools.partial(analysis_kernel, n_e, n_s),
        in_specs=[smem, smem] + [hbm] * 7,
        out_specs=[vmem, vmem],
        out_shape=[pltpu.VMEM(field, f32), pltpu.VMEM(params.shape, f32)],
        scratch_shapes=[
            pltpu.VMEM(u.shape, u.dtype),
            pltpu.VMEM(k.shape, k.dtype),
            pltpu.VMEM((group, cz, nx + 2 * PAD, ny), f32),
            pltpu.VMEM((group, cz, nx + 2 * PAD, ny), f32),
            pltpu.VMEM((group, cz * nx, ny), f32),
            layers, layers, layers, layers,
            pltpu.VMEM((2, half, nx, ny), f32),
            pltpu.VMEM((2, half, nx, ny), bf16),
            pltpu.VMEM((2, half, nx, ny), bf16),
            pltpu.VMEM((1, slots), jnp.int32),
            pltpu.VMEM((own, slots), f32),
            pltpu.VMEM((1, slots), f32),
            pltpu.VMEM((1, slots), f32),
            pltpu.VMEM((2, 1, slots), jnp.int32),
            pltpu.VMEM((2, 2, own, slots), bf16),
            pltpu.VMEM((2, 2, own, slots), bf16),
            pltpu.VMEM((chunks, own, WIDE), f32),
            pltpu.VMEM((n_e, chunks, own, WIDE), f32),
            pltpu.VMEM((n_e,) + params.shape, f32),
            pltpu.VMEM((2 * own, members), f32),
            pltpu.VMEM((n_s, 2 * own, members), f32),
            pltpu.VMEM((own, members), f32),
            pltpu.VMEM((n_e, own, members), f32),
            pltpu.VMEM((own, members), f32),
            pltpu.VMEM((members + own, members), f32),
            dma((9,)),
        ]
        + [dma((2,))] * 4
        + [dma((PARTS, 4))] * 2
        + [dma((PARTS, 2))] * 2
        + [dma((n_e // 2, chunks))] * 4
        + [dma((n_e,))] * 2
        + [dma((n_s,))] * 2
        + [dma((n_e,))] * 2,
        compiler_params=pltpu.CompilerParams(
            collective_id=0,
            has_side_effects=True,
            vmem_limit_bytes=VMEM_BYTES - 4 * math.prod(field) - (512 << 10),
        ),
        name="analysis",
    )(
        position, count, position.reshape(1, -1), noise, values.reshape(1, -1),
        std.reshape(1, -1), params, u, k,
    )


def finish_kernel(pred_ref, post_ref, o_ref, posterior_ref, sem):
    members, cz, nx, ny = o_ref.shape
    block = members // sem.shape[0]
    copies = []
    for i in range(sem.shape[0]):
        for z in range(cz):
            at = pl.ds(i * block, block)
            src = pred_ref.at[at, pl.ds(z * nx, nx)]
            copies.append(pltpu.make_async_copy(src, o_ref.at[at, z], sem.at[i, z]))
    for copy in copies:
        copy.start()
    posterior_ref[...] = post_ref[...]
    for copy in copies:
        copy.wait()


def finish(shape, pred, posterior):
    vmem = pl.BlockSpec(memory_space=pltpu.VMEM)
    return pl.pallas_call(
        finish_kernel,
        in_specs=[vmem, vmem],
        out_specs=[pl.BlockSpec(memory_space=pl.ANY), vmem],
        out_shape=[
            jax.ShapeDtypeStruct(shape, jnp.float32),
            jax.ShapeDtypeStruct(posterior.shape, jnp.float32),
        ],
        scratch_shapes=[pltpu.SemaphoreType.DMA((4, shape[1]))],
        compiler_params=pltpu.CompilerParams(vmem_limit_bytes=20 << 20),
        name="finish",
    )(pred, posterior)


def shards(n_e, n_s, u, k, position, count, values, std, noise, params):
    pred, posterior = analysis(n_e, n_s, position, count, noise, values, std, params, u, k)
    pred, posterior = finish(u.shape, pred, posterior)
    return posterior, pred


def solution(mesh):
    in_specs = (
        P("ens", "space", None, None),
        P("ens", "space", None, None),
        P("space"),
        P("space"),
        P("space"),
        P("space"),
        P("ens", "space"),
        P("ens", "space"),
    )
    out_specs = (P("ens", "space"), P("ens", "space", None, None))
    body = functools.partial(shards, mesh.shape["ens"], mesh.shape["space"])
    return jax.shard_map(body, mesh=mesh, in_specs=in_specs, out_specs=out_specs, check_vma=False)
```

time: 75.8 us -> 69.3 us (0.914)
  Pallas kernels: 74.1 us -> 67.8 us
    pallas_call x1, Pallas kernels: 9.62 us -> 4.16 us  [finish(): pl.pallas_call(finish_kernel, in_specs=[vmem, vmem], out_specs=[pl.BlockS...]
    pallas_call x1, Pallas kernels: 64.5 us -> 63.7 us  [analysis(): pl.pallas_call(functools.partial(analysis_kernel, n_e, n_s), in_specs=[sm...]
where the time goes in v2:
time: 69.3 us; the launch traced here: 69.1 us
  Pallas kernels  67.8 us (98%)
  between operations  1.29 us (2%)
    pallas_call x1, Pallas kernels, analysis(): pl.pallas_call(functools.partial(analysis_kernel, n_e, n_s), in_specs=[sm...  63.7 us
    pallas_call x1, Pallas kernels, finish(): pl.pallas_call(finish_kernel, in_specs=[vmem, vmem], out_specs=[pl.BlockS...  4.16 us

profile of v2, /device:TPU:0, one launch (start us, length us, event | category | flops | bytes accessed | tf_op | source)
XLA Modules:
  0.0 69.1 jit_solution(15565043641116655409)
XLA Ops:
  1.3 63.7 %analysis.1 = (f32[32,520,128]{2,1,0:T(8,128)S(1)}, f32[32,256]{1,0:T(8,128)S(1)}) custom-call(s32[1024]{0:T(1024)} %pos_ref.1, s32[1]{0:T(128)S(6)} %copy.10.count_ref, s32[1,1024]{1,0:T(1,128)} %bitcast.3, f32[32,1024]{1,0:T(8,128)} %noise_hbm.1, f32[1,1024]{1,0:T(1,128)} %bitcast.4, f32[1,1024]{1,0:T(1,128)} %bitcast.5, f32[32,256]{1,0:T(8,128)} %params_hbm.1, ...), custom_call_target="tpu_custom_call" | custom-call | tf_op jit(solution)/shard_map/analysis/pallas_call | solution.py:481
  64.9 4.2 %finish.1 = (f32[32,8,64,128]{3,2,1,0:T(8,128)}, f32[32,256]{1,0:T(8,128)}) custom-call(f32[32,520,128]{2,1,0:T(8,128)S(1)} %get-tuple-element.6.pred_ref, f32[32,256]{1,0:T(8,128)S(1)} %get-tuple-element.7.post_ref), custom_call_target="tpu_custom_call" | custom-call | tf_op jit(solution)/shard_map/finish/pallas_call | solution.py:551

commit v3 on v2

--- a/solution.py
+++ b/solution.py
@@ -13,10 +13,24 @@
 MESH = pl.DeviceIdType.MESH
 VMEM_BYTES = 67043328
 PARTS = 4
+EARLY = 1
 PAD = 8
 WIDE = 256
 f32 = jnp.float32
 bf16 = jnp.bfloat16
+
+
+def squeeze(f):
+    p = f * f
+    p = p * p
+    p = p * p
+    return jnp.where(f < 0.0, -p, p).astype(bf16)
+
+
+def expand(y):
+    y = y.astype(f32)
+    root = jnp.sqrt(jnp.sqrt(jnp.sqrt(jnp.abs(y))))
+    return jnp.where(y < 0.0, -root, root)
 
 
 def pad_rows(fu, fk):
@@ -77,13 +91,13 @@
     lax.fori_loop(0, (hi - lo) // group, members, 0)
 
 
-def solve(gram_ref, cross_ref, work):
-    members = gram_ref.shape[2]
+def solve(gram, cross, work):
+    members = gram.shape[1]
     rows = lax.broadcasted_iota(jnp.int32, (members, members), 0)
     cols = lax.broadcasted_iota(jnp.int32, (members, members), 1)
     lane = lax.broadcasted_iota(jnp.int32, (1, members), 1)
-    work[:members] = gram_ref[...].reshape(members, members) + jnp.where(rows == cols, 1.0, 0.0)
-    work[members:] = cross_ref[...]
+    work[:members] = gram + jnp.where(rows == cols, 1.0, 0.0)
+    work[members:] = cross
 
     pivots = 8
     segments = 4
@@ -130,7 +144,7 @@
     pred, posterior_ref,
     u_ref, k_ref, fu, fk, fy, ulo, klo, uhi, khi, flux, back, ret,
     slots_ref, noise_ref, values_ref, std_ref, asked, answer, got, picked, all_picked,
-    all_params, part, parts, total, gram, cross, work,
+    all_params, own_at, part, pieces, parts, total, sums, work,
     load, send_q, recv_q, send_w, recv_w, send_b, recv_b, send_r, recv_r,
     send_a, recv_a, send_h, recv_h, send_p, recv_p, send_s, recv_s, send_g, recv_g,
 ):
@@ -253,14 +267,14 @@
                 u, k = u_ref[m + shift, z].astype(f32), k_ref[m + shift, z].astype(f32)
                 value = half_step * (k + kn) * (un - u)
                 flux[e, m] = value
-                back[e, m] = value.astype(bf16)
+                back[e, m] = squeeze(value)
             return carry
 
         lax.fori_loop(i * share, (i + 1) * share, one, 0)
         start_pair(returns[i])
 
-    start_pair(bulks[0])
-    start_pair(bulks[1])
+    for i in range(EARLY):
+        start_pair(bulks[i])
     params_copies = [
         send(params_hbm, all_params.at[me_e], send_p.at[d], recv_p.at[d], ens_peer(d))
         for d in range(1, n_e)
@@ -268,7 +282,7 @@
 
     for copy in loads[:2]:
         copy.wait()
-    stencil(0, half, u_ref, k_ref, pred, fu, fk, fy)
+    stencil(0, half // 2, u_ref, k_ref, pred, fu, fk, fy)
     for copy in loads[2:] + small:
         copy.wait()
 
@@ -289,6 +303,10 @@
         g = jnp.dot(layer, hot, preferred_element_type=f32)
         return jnp.sum(jnp.where(mask, g.reshape(own, nx, WIDE), 0.0), axis=1)
 
+    reply = (
+        [remote(answer.at[1], got.at[0], send_w.at[0], recv_w.at[0], above)],
+        [remote(answer.at[0], got.at[1], send_w.at[1], recv_w.at[1], under)],
+    )
     wait_recv_pair(ask)
     for e, z in ((1, top), (0, 0)):
         def answer_chunk(c, carry):
@@ -302,17 +320,15 @@
             return carry
 
         lax.fori_loop(0, chunks, answer_chunk, 0)
-    reply = (
-        [remote(answer.at[1], got.at[0], send_w.at[0], recv_w.at[0], above)],
-        [remote(answer.at[0], got.at[1], send_w.at[1], recv_w.at[1], under)],
-    )
-    start_pair(reply)
-    for i in range(2, PARTS):
+
+        @pl.when((lo_side, hi_side)[e])
+        def _():
+            reply[1 - e][0].start()
+
+    for i in range(EARLY, PARTS):
         start_pair(bulks[i])
     border(0)
-    border(1)
-    stencil(half, own, u_ref, k_ref, pred, fu, fk, fy)
-    wait_recv_pair(reply)
+    stencil(half // 2, own, u_ref, k_ref, pred, fu, fk, fy)
 
     lane = lax.broadcasted_iota(jnp.int32, (own, ny), 1)
     rows = pred.shape[1]
@@ -335,25 +351,14 @@
             across(d, c).wait_recv()
             hand(d, c).start()
 
-    def reading(c, carry):
-        at = columns(c)
-        y, x, z = coordinates(slots_ref[:, at])
+    def reading(c):
+        y, x, z = coordinates(slots_ref[:, columns(c)])
         spot = jnp.where(z == 0, y, jnp.where(z == top, y + ny, -1))
         hot = jnp.where(deep_row == spot, 1.0, 0.0).astype(bf16)
         mask = (x_row == x)[None]
-        u_at, k_at = (
-            pick(
-                jnp.concatenate([ref[:, 0], ref[:, top]], axis=2).reshape(own * nx, 2 * ny),
-                hot, mask,
-            )
-            for ref in (u_ref, k_ref)
-        )
-        change = jnp.zeros((own, WIDE), f32)
-        for e, here, side in ((0, z == 0, lo_side), (1, z == top, hi_side)):
-            other = jnp.logical_and(here, side)
-            u_n = jnp.where(other, got[e, 0, :, at].astype(f32), 0.0)
-            k_n = jnp.where(other, got[e, 1, :, at].astype(f32), 0.0)
-            change += jnp.where(here, half_step * (k_at + k_n) * (u_n - u_at), 0.0)
+        for f, ref in enumerate((u_ref, k_ref)):
+            layer = jnp.concatenate([ref[:, 0], ref[:, top]], axis=2)
+            own_at[f, c] = pick(layer.reshape(own * nx, 2 * ny), hot, mask)
         for h in range(0, WIDE, ny):
             def step(s, acc):
                 for i in range(unroll):
@@ -366,19 +371,52 @@
 
             unroll = ny // 2
             acc = lax.fori_loop(0, ny // unroll, step, jnp.zeros((own, ny), f32))
-            picked[c, :, h : h + ny] = acc + change[:, h : h + ny]
-        all_picked[me_e, c] = picked[c]
+            picked[c, :, h : h + ny] = acc
+
+    def complete(c):
+        at = columns(c)
+        _, _, z = coordinates(slots_ref[:, at])
+        u_at, k_at = own_at[0, c], own_at[1, c]
+        value = picked[c]
+        for e, here, side in ((0, z == 0, lo_side), (1, z == top, hi_side)):
+            other = jnp.logical_and(here, side)
+            u_n = jnp.where(other, got[e, 0, :, at].astype(f32), 0.0)
+            k_n = jnp.where(other, got[e, 1, :, at].astype(f32), 0.0)
+            value += jnp.where(here, half_step * (k_at + k_n) * (u_n - u_at), 0.0)
+        picked[c] = value
+        all_picked[me_e, c] = value
         hand(0, c).start()
         for d in range(1, hops):
             across(d, c).start()
 
+    ahead = chunks // 2
+
+    def first_readings(c, carry):
+        reading(c)
+        return carry
+
+    lax.fori_loop(0, ahead, first_readings, 0)
+    wait_recv_pair(reply)
+
+    def more_readings(c, carry):
+        complete(c)
+        reading(c + ahead)
+
         @pl.when(c > 0)
         def _():
             relay(c - 1)
 
         return carry
 
-    lax.fori_loop(0, chunks, reading, 0)
+    lax.fori_loop(0, chunks - ahead, more_readings, 0)
+    border(1)
+
+    def last_readings(c, carry):
+        complete(c)
+        relay(c - 1)
+        return carry
+
+    lax.fori_loop(chunks - ahead, chunks, last_readings, 0)
     border(2)
     relay(chunks - 1)
 
@@ -396,7 +434,7 @@
         everyone = all_picked[:, c].reshape(members, WIDE)
         centre = jnp.sum(everyone, axis=0, keepdims=True) / members
         spread = (everyone - centre) * inverse
-        left = jnp.concatenate([(mine - centre) * inverse, misfit], axis=0)
+        left = jnp.concatenate([spread, misfit], axis=0)
         part[...] += lax.dot_general(
             left, spread, (((1,), (1,)), ((), ())),
             precision=HI, preferred_element_type=f32,
@@ -404,22 +442,26 @@
         return carry
 
     lax.fori_loop(0, chunks, product, 0)
-    space_copies = [
-        send(part, parts.at[d], send_s.at[d], recv_s.at[d], space_peer(d)) for d in range(1, n_s)
-    ]
+    grams, crosses = members // n_s, own // n_s
+    pieces[:, :grams] = part[:members].reshape(n_s, grams, members)
+    for i in range(n_s):
+        pieces[i, grams : grams + crosses] = part[members + i * crosses : members + (i + 1) * crosses]
+    scatter = []
+    for d in range(1, n_s):
+        src = pieces.at[lax.rem(me_s + d, n_s)]
+        scatter.append(send(src, parts.at[d], send_s.at[d], recv_s.at[d], space_peer(d)))
     for i in range(3, PARTS):
         border(i)
-    acc = part[...]
+    acc = pieces[me_s]
     for d in range(1, n_s):
-        space_copies[d - 1].wait()
+        scatter[d - 1].wait()
         acc += parts[d]
-    total[...] = acc[:own]
-    gram_copies = [
-        send(total, gram.at[me_e], send_g.at[d], recv_g.at[d], ens_peer(d))
-        for d in range(1, n_e)
+    total[...] = acc
+    sums[me_s] = acc
+    gather = [
+        send(total, sums.at[me_s], send_g.at[d], recv_g.at[d], space_peer(d))
+        for d in range(1, n_s)
     ]
-    gram[me_e] = acc[:own]
-    cross[...] = acc[own:]
 
     def add_flux(m, carry):
         bottom, upper = pl.ds(0, nx), pl.ds(top * nx, nx)
@@ -428,8 +470,10 @@
         return carry
 
     lax.fori_loop(0, half, add_flux, 0)
-    for copy in gram_copies:
+    for copy in gather:
         copy.wait()
+    gram = sums[:, :grams].reshape(members, members)
+    cross = jnp.concatenate([sums[i, grams : grams + crosses] for i in range(n_s)], axis=0)
     for copy in params_copies:
         copy.wait()
     weights = solve(gram, cross, work)
@@ -444,7 +488,7 @@
         for e, z, shift, side in ((0, 0, half, lo_side), (1, top, 0, hi_side)):
             at = pl.ds(z * nx, nx)
             u, k = u_ref[m + shift, z].astype(f32), k_ref[m + shift, z].astype(f32)
-            lost = jnp.where(side, ret[e, m].astype(f32), half_step * k * u)
+            lost = jnp.where(side, expand(ret[e, m]), half_step * k * u)
             pred[m + shift, at] = pred[m + shift, at] - lost
         return carry
 
@@ -471,6 +515,7 @@
     chunks = slots // WIDE
     members = own * n_e
     half = own // 2
+    piece = members // n_s + 8 * pl.cdiv(own // n_s, 8)
     vmem = pl.BlockSpec(memory_space=pltpu.VMEM)
     smem = pl.BlockSpec(memory_space=pltpu.SMEM)
     hbm = pl.BlockSpec(memory_space=pltpu.HBM)
@@ -503,11 +548,12 @@
             pltpu.VMEM((chunks, own, WIDE), f32),
             pltpu.VMEM((n_e, chunks, own, WIDE), f32),
             pltpu.VMEM((n_e,) + params.shape, f32),
-            pltpu.VMEM((2 * own, members), f32),
-            pltpu.VMEM((n_s, 2 * own, members), f32),
-            pltpu.VMEM((own, members), f32),
-            pltpu.VMEM((n_e, own, members), f32),
-            pltpu.VMEM((own, members), f32),
+            pltpu.VMEM((2, chunks, own, WIDE), f32),
+            pltpu.VMEM((members + own, members), f32),
+            pltpu.VMEM((n_s, piece, members), f32),
+            pltpu.VMEM((n_s, piece, members), f32),
+            pltpu.VMEM((piece, members), f32),
+            pltpu.VMEM((n_s, piece, members), f32),
             pltpu.VMEM((members + own, members), f32),
             dma((9,)),
         ]
@@ -516,8 +562,7 @@
         + [dma((PARTS, 2))] * 2
         + [dma((n_e // 2, chunks))] * 4
         + [dma((n_e,))] * 2
-        + [dma((n_s,))] * 2
-        + [dma((n_e,))] * 2,
+        + [dma((n_s,))] * 4,
         compiler_params=pltpu.CompilerParams(
             collective_id=0,
             has_side_effects=True,

time: 69.3 us -> 66.6 us (0.961)
  Pallas kernels: 67.8 us -> 65.2 us
    pallas_call x1, Pallas kernels: 63.7 us -> 61 us  [analysis(): pl.pallas_call(functools.partial(analysis_kernel, n_e, n_s), in_specs=[sm...]
where the time goes in v3:
time: 66.6 us; the launch traced here: 66.4 us
  Pallas kernels  65.2 us (98%)
  between operations  1.29 us (2%)
    pallas_call x1, Pallas kernels, analysis(): pl.pallas_call(functools.partial(analysis_kernel, n_e, n_s), in_specs=[sm...  61 us
    pallas_call x1, Pallas kernels, finish(): pl.pallas_call(finish_kernel, in_specs=[vmem, vmem], out_specs=[pl.BlockS...  4.16 us

profile of v3, /device:TPU:0, one launch (start us, length us, event | category | flops | bytes accessed | tf_op | source)
XLA Modules:
  0.0 66.4 jit_solution(17328886022730294572)
XLA Ops:
  1.3 61.0 %analysis.1 = (f32[32,520,128]{2,1,0:T(8,128)S(1)}, f32[32,256]{1,0:T(8,128)S(1)}) custom-call(s32[1024]{0:T(1024)} %pos_ref.1, s32[1]{0:T(128)S(6)} %copy.10.count_ref, s32[1,1024]{1,0:T(1,128)} %bitcast.3, f32[32,1024]{1,0:T(8,128)} %noise_hbm.1, f32[1,1024]{1,0:T(1,128)} %bitcast.4, f32[1,1024]{1,0:T(1,128)} %bitcast.5, f32[32,256]{1,0:T(8,128)} %params_hbm.1, ...), custom_call_target="tpu_custom_call" | custom-call | tf_op jit(solution)/shard_map/analysis/pallas_call | solution.py:526
  62.3 4.2 %finish.1 = (f32[32,8,64,128]{3,2,1,0:T(8,128)}, f32[32,256]{1,0:T(8,128)}) custom-call(f32[32,520,128]{2,1,0:T(8,128)S(1)} %get-tuple-element.6.pred_ref, f32[32,256]{1,0:T(8,128)S(1)} %get-tuple-element.7.post_ref), custom_call_target="tpu_custom_call" | custom-call | tf_op jit(solution)/shard_map/finish/pallas_call | solution.py:596

commit v4 on v3

--- a/solution.py
+++ b/solution.py
@@ -14,6 +14,11 @@
 VMEM_BYTES = 67043328
 PARTS = 4
 EARLY = 1
+LATE = 3
+FIRST = 1
+BEFORE = 2
+AHEAD = 3
+MIDDLE = 0
 PAD = 8
 WIDE = 256
 f32 = jnp.float32
@@ -103,7 +108,7 @@
     segments = 4
     span = members // segments
 
-    def step(lo, s, diagonal):
+    def step(lo, s, carry):
         first = lo + s * pivots
         t = work[lo:]
         here = [lane == first + i for i in range(pivots)]
@@ -115,27 +120,27 @@
             [jnp.sum(jnp.where(here[j], rows[i], 0.0), axis=1, keepdims=True) for j in range(pivots)]
             for i in range(pivots)
         ]
+        rows = [rows[i] - jnp.where(here[i], 1.0, 0.0) for i in range(pivots)]
         for i in range(pivots):
-            pivot = corner[i][i]
-            diagonal = jnp.where(here[i], pivot, diagonal)
-            inverse = 1.0 / pivot
-            factor = jnp.where(here[i], 0.0, rows[i] * inverse)
-            t = t - columns[i] * factor
+            inverse = 1.0 / corner[i][i]
+            rows[i] = rows[i] * inverse
             for j in range(i + 1, pivots):
-                ratio = corner[i][j] * inverse
-                columns[j] = columns[j] - columns[i] * ratio
-                rows[j] = rows[j] - corner[j][i] * factor
-                for l in range(i + 1, pivots):
-                    corner[l][j] = corner[l][j] - corner[l][i] * ratio
+                corner[i][j] = corner[i][j] * inverse
+            for l in range(i + 1, pivots):
+                rows[l] = rows[l] - corner[l][i] * rows[i]
+                for j in range(i + 1, pivots):
+                    corner[l][j] = corner[l][j] - corner[l][i] * corner[i][j]
+        for i in range(pivots - 1, -1, -1):
+            for j in range(i + 1, pivots):
+                rows[i] = rows[i] - corner[i][j] * rows[j]
+        for i in range(pivots):
+            t = t - columns[i] * rows[i]
         work[lo:] = t
-        return diagonal
-
-    diagonal = jnp.ones((1, members), jnp.float32)
+        return carry
+
     for part in range(segments):
-        diagonal = lax.fori_loop(
-            0, span // pivots, functools.partial(step, part * span), diagonal
-        )
-    return work[members:] / diagonal
+        lax.fori_loop(0, span // pivots, functools.partial(step, part * span), 0)
+    return work[members:]
 
 
 def analysis_kernel(
@@ -145,7 +150,7 @@
     u_ref, k_ref, fu, fk, fy, ulo, klo, uhi, khi, flux, back, ret,
     slots_ref, noise_ref, values_ref, std_ref, asked, answer, got, picked, all_picked,
     all_params, own_at, part, pieces, parts, total, sums, work,
-    load, send_q, recv_q, send_w, recv_w, send_b, recv_b, send_r, recv_r,
+    gate, load, send_q, recv_q, send_w, recv_w, send_b, recv_b, send_r, recv_r,
     send_a, recv_a, send_h, recv_h, send_p, recv_p, send_s, recv_s, send_g, recv_g,
 ):
     own, cz, nx, ny = u_ref.shape
@@ -164,19 +169,18 @@
         copy.start()
         return copy
 
-    first, second = pl.ds(0, half), pl.ds(half, half)
-    loads = [
-        local(u_hbm.at[first], u_ref.at[first], 0),
-        local(k_hbm.at[first], k_ref.at[first], 1),
-        local(u_hbm.at[second], u_ref.at[second], 2),
-        local(k_hbm.at[second], k_ref.at[second], 3),
-    ]
+    quarter = own // 4
+    loads = []
+    for i in range(4):
+        at = pl.ds(i * quarter, quarter)
+        loads.append(local(u_hbm.at[at], u_ref.at[at], 2 * i))
+        loads.append(local(k_hbm.at[at], k_ref.at[at], 2 * i + 1))
     small = [
-        local(slots_hbm, slots_ref, 4),
-        local(noise_hbm, noise_ref, 5),
-        local(values_hbm, values_ref, 6),
-        local(std_hbm, std_ref, 7),
-        local(params_hbm, all_params.at[me_e], 8),
+        local(slots_hbm, slots_ref, 8),
+        local(noise_hbm, noise_ref, 9),
+        local(values_hbm, values_ref, 10),
+        local(std_hbm, std_ref, 11),
+        local(params_hbm, all_params.at[me_e], 12),
     ]
 
     def ens_peer(d):
@@ -188,10 +192,31 @@
     barrier = pltpu.get_barrier_semaphore()
     for d in range(1, n_e):
         pl.semaphore_signal(barrier, inc=1, device_id=ens_peer(d), device_id_type=MESH)
-    for d in range(1, n_s):
-        pl.semaphore_signal(barrier, inc=1, device_id=space_peer(d), device_id_type=MESH)
+
+    def at_distance(d, what):
+        for there, peer in ((me_s >= d, me_s - d), (me_s + d < n_s, me_s + d)):
+            @pl.when(there)
+            def _():
+                what((me_e, peer))
+
+    def signal(sem, peer):
+        pl.semaphore_signal(sem, inc=1, device_id=peer, device_id_type=MESH)
+
+    at_distance(1, functools.partial(signal, barrier))
     pad_rows(fu, fk)
-    pl.semaphore_wait(barrier, n_e + n_s - 2)
+    def peers_at(d):
+        return (me_s >= d).astype(jnp.int32) + (me_s + d < n_s).astype(jnp.int32)
+
+    pl.semaphore_wait(barrier, n_e - 1 + peers_at(1))
+
+    def gate_signal(r):
+        at_distance(1 << r, functools.partial(signal, gate.at[r]))
+
+    def gate_wait(r):
+        pl.semaphore_wait(gate.at[r], peers_at(1 << r))
+
+    rounds = gate.shape[0]
+    gate_signal(0)
 
     def remote(src, dst, ssem, rsem, peer):
         return pltpu.make_async_remote_copy(
@@ -271,7 +296,6 @@
             return carry
 
         lax.fori_loop(i * share, (i + 1) * share, one, 0)
-        start_pair(returns[i])
 
     for i in range(EARLY):
         start_pair(bulks[i])
@@ -280,11 +304,16 @@
         for d in range(1, n_e)
     ]
 
-    for copy in loads[:2]:
+    def quarter_stencil(i):
+        stencil(i * quarter, (i + 1) * quarter, u_ref, k_ref, pred, fu, fk, fy)
+
+    for i in range(BEFORE):
+        for copy in loads[2 * i : 2 * i + 2]:
+            copy.wait()
+        quarter_stencil(i)
+    for copy in loads[2 * BEFORE :] + small:
         copy.wait()
-    stencil(0, half // 2, u_ref, k_ref, pred, fu, fk, fy)
-    for copy in loads[2:] + small:
-        copy.wait()
+    gate_wait(0)
 
     lane_row = lax.broadcasted_iota(jnp.int32, (ny, WIDE), 0)
     deep_row = lax.broadcasted_iota(jnp.int32, (2 * ny, WIDE), 0)
@@ -325,10 +354,17 @@
         def _():
             reply[1 - e][0].start()
 
-    for i in range(EARLY, PARTS):
+    for i in range(EARLY, LATE):
         start_pair(bulks[i])
+    for r in range(1, rounds):
+        gate_signal(r)
+        if r < rounds - 1:
+            gate_wait(r)
+    for i in range(BEFORE, 4):
+        quarter_stencil(i)
     border(0)
-    stencil(half // 2, own, u_ref, k_ref, pred, fu, fk, fy)
+    for i in range(FIRST):
+        start_pair(returns[i])
 
     lane = lax.broadcasted_iota(jnp.int32, (own, ny), 1)
     rows = pred.shape[1]
@@ -389,7 +425,7 @@
         for d in range(1, hops):
             across(d, c).start()
 
-    ahead = chunks // 2
+    ahead = min(AHEAD, chunks)
 
     def first_readings(c, carry):
         reading(c)
@@ -399,8 +435,8 @@
     wait_recv_pair(reply)
 
     def more_readings(c, carry):
+        reading(c + ahead)
         complete(c)
-        reading(c + ahead)
 
         @pl.when(c > 0)
         def _():
@@ -409,15 +445,16 @@
         return carry
 
     lax.fori_loop(0, chunks - ahead, more_readings, 0)
-    border(1)
-
     def last_readings(c, carry):
         complete(c)
-        relay(c - 1)
+
+        @pl.when(c > 0)
+        def _():
+            relay(c - 1)
+
         return carry
 
     lax.fori_loop(chunks - ahead, chunks, last_readings, 0)
-    border(2)
     relay(chunks - 1)
 
     part[...] = jnp.zeros_like(part)
@@ -446,12 +483,17 @@
     pieces[:, :grams] = part[:members].reshape(n_s, grams, members)
     for i in range(n_s):
         pieces[i, grams : grams + crosses] = part[members + i * crosses : members + (i + 1) * crosses]
+    gate_wait(rounds - 1)
     scatter = []
     for d in range(1, n_s):
         src = pieces.at[lax.rem(me_s + d, n_s)]
         scatter.append(send(src, parts.at[d], send_s.at[d], recv_s.at[d], space_peer(d)))
-    for i in range(3, PARTS):
+    for i in range(LATE, PARTS):
+        start_pair(bulks[i])
+    for i in range(1, LATE):
         border(i)
+    for i in range(FIRST, FIRST + MIDDLE):
+        start_pair(returns[i])
     acc = pieces[me_s]
     for d in range(1, n_s):
         scatter[d - 1].wait()
@@ -462,6 +504,11 @@
         send(total, sums.at[me_s], send_g.at[d], recv_g.at[d], space_peer(d))
         for d in range(1, n_s)
     ]
+    for i in range(FIRST + MIDDLE, LATE):
+        start_pair(returns[i])
+    for i in range(LATE, PARTS):
+        border(i)
+        start_pair(returns[i])
 
     def add_flux(m, carry):
         bottom, upper = pl.ds(0, nx), pl.ds(top * nx, nx)
@@ -555,7 +602,8 @@
             pltpu.VMEM((piece, members), f32),
             pltpu.VMEM((n_s, piece, members), f32),
             pltpu.VMEM((members + own, members), f32),
-            dma((9,)),
+            pltpu.SemaphoreType.REGULAR((max(1, (n_s - 1).bit_length()),)),
+            dma((13,)),
         ]
         + [dma((2,))] * 4
         + [dma((PARTS, 4))] * 2

time: 66.6 us -> 62.1 us (0.932)
  the two profiles are of different devices: /device:TPU:0 before, /device:TPU:16 now
where the time goes in v4:
time: 62.1 us; the launch traced here: 61.9 us
  Pallas kernels  60.6 us (98%)
  between operations  1.29 us (2%)
    pallas_call x1, Pallas kernels, analysis(): pl.pallas_call(functools.partial(analysis_kernel, n_e, n_s), in_specs=[sm...  56.4 us
    pallas_call x1, Pallas kernels, finish(): pl.pallas_call(finish_kernel, in_specs=[vmem, vmem], out_specs=[pl.BlockS...  4.16 us

profile of v4, /device:TPU:16, one launch (start us, length us, event | category | flops | bytes accessed | tf_op | source)
XLA Modules:
  0.0 61.9 jit_solution(4304661191104669842)
XLA Ops:
  1.3 56.4 %analysis.1 = (f32[32,520,128]{2,1,0:T(8,128)S(1)}, f32[32,256]{1,0:T(8,128)S(1)}) custom-call(s32[1024]{0:T(1024)} %pos_ref.1, s32[1]{0:T(128)S(6)} %copy.10.count_ref, s32[1,1024]{1,0:T(1,128)} %bitcast.3, f32[32,1024]{1,0:T(8,128)} %noise_hbm.1, f32[1,1024]{1,0:T(1,128)} %bitcast.4, f32[1,1024]{1,0:T(1,128)} %bitcast.5, f32[32,256]{1,0:T(8,128)} %params_hbm.1, ...), custom_call_target="tpu_custom_call" | custom-call | tf_op jit(solution)/shard_map/analysis/pallas_call | solution.py:573
  57.7 4.2 %finish.1 = (f32[32,8,64,128]{3,2,1,0:T(8,128)}, f32[32,256]{1,0:T(8,128)}) custom-call(f32[32,520,128]{2,1,0:T(8,128)S(1)} %get-tuple-element.6.pred_ref, f32[32,256]{1,0:T(8,128)S(1)} %get-tuple-element.7.post_ref), custom_call_target="tpu_custom_call" | custom-call | tf_op jit(solution)/shard_map/finish/pallas_call | solution.py:644

commit v5 on v4

--- a/solution.py
+++ b/solution.py
@@ -12,13 +12,15 @@
 HI = lax.Precision.HIGHEST
 MESH = pl.DeviceIdType.MESH
 VMEM_BYTES = 67043328
-PARTS = 4
+PARTS = 8
 EARLY = 1
-LATE = 3
+LATE = 6
 FIRST = 1
 BEFORE = 2
 AHEAD = 3
 MIDDLE = 0
+ADDED = 4
+BACK = 1
 PAD = 8
 WIDE = 256
 f32 = jnp.float32
@@ -34,7 +36,8 @@
 
 def expand(y):
     y = y.astype(f32)
-    root = jnp.sqrt(jnp.sqrt(jnp.sqrt(jnp.abs(y))))
+    quarter = lax.rsqrt(lax.rsqrt(jnp.abs(y)))
+    root = jnp.where(y == 0.0, 0.0, quarter * lax.rsqrt(quarter))
     return jnp.where(y < 0.0, -root, root)
 
 
@@ -144,12 +147,12 @@
 
 
 def analysis_kernel(
-    n_e, n_s, pos_ref, count_ref, slots_hbm, noise_hbm, values_hbm, std_hbm, params_hbm,
+    n_e, n_s, pos_hbm, count_hbm, slots_hbm, noise_hbm, values_hbm, std_hbm, params_hbm,
     u_hbm, k_hbm,
     pred, posterior_ref,
     u_ref, k_ref, fu, fk, fy, ulo, klo, uhi, khi, flux, back, ret,
-    slots_ref, noise_ref, values_ref, std_ref, asked, answer, got, picked, all_picked,
-    all_params, own_at, part, pieces, parts, total, sums, work,
+    pos_ref, count_ref, slots_ref, noise_ref, values_ref, std_ref, asked, answer, got, picked, all_picked,
+    all_params, own_at, part, pieces, parts, total, sums, work, anomaly,
     gate, load, send_q, recv_q, send_w, recv_w, send_b, recv_b, send_r, recv_r,
     send_a, recv_a, send_h, recv_h, send_p, recv_p, send_s, recv_s, send_g, recv_g,
 ):
@@ -177,6 +180,8 @@
         loads.append(local(k_hbm.at[at], k_ref.at[at], 2 * i + 1))
     small = [
         local(slots_hbm, slots_ref, 8),
+        local(pos_hbm, pos_ref, 13),
+        local(count_hbm, count_ref, 14),
         local(noise_hbm, noise_ref, 9),
         local(values_hbm, values_ref, 10),
         local(std_hbm, std_ref, 11),
@@ -315,7 +320,6 @@
         copy.wait()
     gate_wait(0)
 
-    lane_row = lax.broadcasted_iota(jnp.int32, (ny, WIDE), 0)
     deep_row = lax.broadcasted_iota(jnp.int32, (2 * ny, WIDE), 0)
     x_row = lax.broadcasted_iota(jnp.int32, (nx, WIDE), 0)
     bits_y, bits_x = int(math.log2(ny)), int(math.log2(nx))
@@ -329,8 +333,9 @@
         return pl.ds(pl.multiple_of(c * WIDE, WIDE), WIDE)
 
     def pick(layer, hot, mask):
-        g = jnp.dot(layer, hot, preferred_element_type=f32)
-        return jnp.sum(jnp.where(mask, g.reshape(own, nx, WIDE), 0.0), axis=1)
+        lines = layer.shape[1]
+        g = jnp.dot(layer.reshape(own * lines, 2 * ny), hot, preferred_element_type=f32)
+        return jnp.sum(jnp.where(mask, g.reshape(own, lines, WIDE), 0.0), axis=1)
 
     reply = (
         [remote(answer.at[1], got.at[0], send_w.at[0], recv_w.at[0], above)],
@@ -341,10 +346,11 @@
         def answer_chunk(c, carry):
             at = columns(c)
             y, x, _ = coordinates(asked[e, :, at])
-            hot = jnp.where(lane_row == y, 1.0, 0.0).astype(bf16)
-            mask = (x_row == x)[None]
+            spot = jnp.where(x < nx // 2, y, y + ny)
+            hot = jnp.where(deep_row == spot, 1.0, 0.0).astype(bf16)
+            mask = (x_row[: nx // 2] == (x & (nx // 2 - 1)))[None]
             for f, ref in enumerate((u_ref, k_ref)):
-                layer = ref[:, z].reshape(own * nx, ny)
+                layer = jnp.concatenate([ref[:, z, : nx // 2], ref[:, z, nx // 2 :]], axis=2)
                 answer[e, f, :, at] = pick(layer, hot, mask).astype(bf16)
             return carry
 
@@ -362,8 +368,8 @@
             gate_wait(r)
     for i in range(BEFORE, 4):
         quarter_stencil(i)
-    border(0)
     for i in range(FIRST):
+        border(i)
         start_pair(returns[i])
 
     lane = lax.broadcasted_iota(jnp.int32, (own, ny), 1)
@@ -394,7 +400,7 @@
         mask = (x_row == x)[None]
         for f, ref in enumerate((u_ref, k_ref)):
             layer = jnp.concatenate([ref[:, 0], ref[:, top]], axis=2)
-            own_at[f, c] = pick(layer.reshape(own * nx, 2 * ny), hot, mask)
+            own_at[f, c] = pick(layer, hot, mask)
         for h in range(0, WIDE, ny):
             def step(s, acc):
                 for i in range(unroll):
@@ -464,7 +470,7 @@
         for d in range(hops):
             hand(d, c).wait_recv()
         mine = picked[c]
-        live = lax.broadcasted_iota(jnp.int32, (1, WIDE), 1) + c * WIDE < count_ref[0]
+        live = lax.broadcasted_iota(jnp.int32, (1, WIDE), 1) + c * WIDE < count_ref[...]
         std = std_ref[:, at]
         inverse = jnp.where(live, 1.0 / (std * scale), 0.0)
         misfit = jnp.where(live, (values_ref[:, at] - mine) / std + noise_ref[:, at], 0.0)
@@ -483,6 +489,24 @@
     pieces[:, :grams] = part[:members].reshape(n_s, grams, members)
     for i in range(n_s):
         pieces[i, grams : grams + crosses] = part[members + i * crosses : members + (i + 1) * crosses]
+    def add_flux(m, carry):
+        bottom, upper = pl.ds(0, nx), pl.ds(top * nx, nx)
+        pred[m, bottom] = pred[m, bottom] + flux[0, m]
+        pred[m + half, upper] = pred[m + half, upper] + flux[1, m]
+        return carry
+
+    def add_returned(m, carry):
+        for e, z, shift, side in ((0, 0, half, lo_side), (1, top, 0, hi_side)):
+            at = pl.ds(z * nx, nx)
+            u, k = u_ref[m + shift, z].astype(f32), k_ref[m + shift, z].astype(f32)
+            lost = jnp.where(side, expand(ret[e, m]), half_step * k * u)
+            pred[m + shift, at] = pred[m + shift, at] - lost
+        return carry
+
+    def finish_returned(i):
+        wait_recv_pair(returns[i])
+        lax.fori_loop(i * share, (i + 1) * share, add_returned, 0)
+
     gate_wait(rounds - 1)
     scatter = []
     for d in range(1, n_s):
@@ -490,10 +514,17 @@
         scatter.append(send(src, parts.at[d], send_s.at[d], recv_s.at[d], space_peer(d)))
     for i in range(LATE, PARTS):
         start_pair(bulks[i])
-    for i in range(1, LATE):
+    for i in range(FIRST, LATE):
         border(i)
     for i in range(FIRST, FIRST + MIDDLE):
         start_pair(returns[i])
+    for copy in params_copies:
+        copy.wait()
+    everyones = all_params[...].reshape(members, -1)
+    centre = jnp.sum(everyones, axis=0, keepdims=True) / members
+    anomaly[...] = (everyones - centre) / scale
+    for i in range(ADDED):
+        lax.fori_loop(i * share, (i + 1) * share, add_flux, 0)
     acc = pieces[me_s]
     for d in range(1, n_s):
         scatter[d - 1].wait()
@@ -510,38 +541,21 @@
         border(i)
         start_pair(returns[i])
 
-    def add_flux(m, carry):
-        bottom, upper = pl.ds(0, nx), pl.ds(top * nx, nx)
-        pred[m, bottom] = pred[m, bottom] + flux[0, m]
-        pred[m + half, upper] = pred[m + half, upper] + flux[1, m]
-        return carry
-
-    lax.fori_loop(0, half, add_flux, 0)
+    for i in range(ADDED, PARTS):
+        lax.fori_loop(i * share, (i + 1) * share, add_flux, 0)
+    for i in range(BACK):
+        finish_returned(i)
     for copy in gather:
         copy.wait()
     gram = sums[:, :grams].reshape(members, members)
     cross = jnp.concatenate([sums[i, grams : grams + crosses] for i in range(n_s)], axis=0)
-    for copy in params_copies:
-        copy.wait()
     weights = solve(gram, cross, work)
-    everyones = all_params[...].reshape(members, -1)
-    centre = jnp.sum(everyones, axis=0, keepdims=True) / members
-    anomaly = (everyones - centre) / math.sqrt(members - 1.0)
     posterior_ref[...] = all_params[me_e] + jnp.dot(
-        weights, anomaly, precision=HI, preferred_element_type=f32
+        weights, anomaly[...], precision=HI, preferred_element_type=f32
     )
 
-    def add_returned(m, carry):
-        for e, z, shift, side in ((0, 0, half, lo_side), (1, top, 0, hi_side)):
-            at = pl.ds(z * nx, nx)
-            u, k = u_ref[m + shift, z].astype(f32), k_ref[m + shift, z].astype(f32)
-            lost = jnp.where(side, expand(ret[e, m]), half_step * k * u)
-            pred[m + shift, at] = pred[m + shift, at] - lost
-        return carry
-
-    for i in range(PARTS):
-        wait_recv_pair(returns[i])
-        lax.fori_loop(i * share, (i + 1) * share, add_returned, 0)
+    for i in range(BACK, PARTS):
+        finish_returned(i)
 
     for pair in [ask, reply] + bulks + returns:
         wait_send_pair(pair)
@@ -564,7 +578,6 @@
     half = own // 2
     piece = members // n_s + 8 * pl.cdiv(own // n_s, 8)
     vmem = pl.BlockSpec(memory_space=pltpu.VMEM)
-    smem = pl.BlockSpec(memory_space=pltpu.SMEM)
     hbm = pl.BlockSpec(memory_space=pltpu.HBM)
     dma = pltpu.SemaphoreType.DMA
     field = (own, cz * nx + PAD, ny)
@@ -572,7 +585,7 @@
     group = 4
     return pl.pallas_call(
         functools.partial(analysis_kernel, n_e, n_s),
-        in_specs=[smem, smem] + [hbm] * 7,
+        in_specs=[hbm] * 9,
         out_specs=[vmem, vmem],
         out_shape=[pltpu.VMEM(field, f32), pltpu.VMEM(params.shape, f32)],
         scratch_shapes=[
@@ -585,6 +598,8 @@
             pltpu.VMEM((2, half, nx, ny), f32),
             pltpu.VMEM((2, half, nx, ny), bf16),
             pltpu.VMEM((2, half, nx, ny), bf16),
+            pltpu.SMEM((slots,), jnp.int32),
+            pltpu.VMEM((1, 1), jnp.int32),
             pltpu.VMEM((1, slots), jnp.int32),
             pltpu.VMEM((own, slots), f32),
             pltpu.VMEM((1, slots), f32),
@@ -602,8 +617,9 @@
             pltpu.VMEM((piece, members), f32),
             pltpu.VMEM((n_s, piece, members), f32),
             pltpu.VMEM((members + own, members), f32),
+            pltpu.VMEM((members, params.shape[1]), f32),
             pltpu.SemaphoreType.REGULAR((max(1, (n_s - 1).bit_length()),)),
-            dma((13,)),
+            dma((15,)),
         ]
         + [dma((2,))] * 4
         + [dma((PARTS, 4))] * 2
@@ -618,20 +634,20 @@
         ),
         name="analysis",
     )(
-        position, count, position.reshape(1, -1), noise, values.reshape(1, -1),
+        position, count.reshape(1, 1), position.reshape(1, -1), noise, values.reshape(1, -1),
         std.reshape(1, -1), params, u, k,
     )
 
 
 def finish_kernel(pred_ref, post_ref, o_ref, posterior_ref, sem):
-    members, cz, nx, ny = o_ref.shape
+    members, cells = o_ref.shape[:2]
     block = members // sem.shape[0]
-    copies = []
-    for i in range(sem.shape[0]):
-        for z in range(cz):
-            at = pl.ds(i * block, block)
-            src = pred_ref.at[at, pl.ds(z * nx, nx)]
-            copies.append(pltpu.make_async_copy(src, o_ref.at[at, z], sem.at[i, z]))
+
+    def copy_of(i):
+        at = pl.ds(i * block, block)
+        return pltpu.make_async_copy(pred_ref.at[at, pl.ds(0, cells)], o_ref.at[at], sem.at[i])
+
+    copies = [copy_of(i) for i in range(sem.shape[0])]
     for copy in copies:
         copy.start()
     posterior_ref[...] = post_ref[...]
@@ -641,18 +657,20 @@
 
 def finish(shape, pred, posterior):
     vmem = pl.BlockSpec(memory_space=pltpu.VMEM)
-    return pl.pallas_call(
+    flat = (shape[0], shape[1] * shape[2], shape[3])
+    pred, posterior = pl.pallas_call(
         finish_kernel,
         in_specs=[vmem, vmem],
         out_specs=[pl.BlockSpec(memory_space=pl.ANY), vmem],
         out_shape=[
-            jax.ShapeDtypeStruct(shape, jnp.float32),
-            jax.ShapeDtypeStruct(posterior.shape, jnp.float32),
+            jax.ShapeDtypeStruct(flat, f32),
+            jax.ShapeDtypeStruct(posterior.shape, f32),
         ],
-        scratch_shapes=[pltpu.SemaphoreType.DMA((4, shape[1]))],
+        scratch_shapes=[pltpu.SemaphoreType.DMA((16,))],
         compiler_params=pltpu.CompilerParams(vmem_limit_bytes=20 << 20),
         name="finish",
     )(pred, posterior)
+    return pred.reshape(shape), posterior
 
 
 def shards(n_e, n_s, u, k, position, count, values, std, noise, params):

time: 62.1 us -> 60.2 us (0.969)
  the two profiles are of different devices: /device:TPU:16 before, /device:TPU:8 now
where the time goes in v5:
time: 60.2 us; the launch traced here: 60 us
  Pallas kernels  58.7 us (98%)
  between operations  1.29 us (2%)
    pallas_call x1, Pallas kernels, analysis(): pl.pallas_call(functools.partial(analysis_kernel, n_e, n_s), in_specs=[hb...  54.7 us
    pallas_call x1, Pallas kernels, finish(): pl.pallas_call(finish_kernel, in_specs=[vmem, vmem], out_specs=[pl.BlockS...  4.03 us

profile of v5, /device:TPU:8, one launch (start us, length us, event | category | flops | bytes accessed | tf_op | source)
XLA Modules:
  0.0 60.0 jit_solution(18431855516811128720)
XLA Ops:
  1.3 54.7 %analysis.1 = (f32[32,520,128]{2,1,0:T(8,128)S(1)}, f32[32,256]{1,0:T(8,128)S(1)}) custom-call(s32[1024]{0:T(1024)} %pos_hbm.1, s32[1,1]{1,0:T(1,128)} %bitcast.5.count_hbm, s32[1,1024]{1,0:T(1,128)} %bitcast.6, f32[32,1024]{1,0:T(8,128)} %noise_hbm.1, f32[1,1024]{1,0:T(1,128)} %bitcast.7, f32[1,1024]{1,0:T(1,128)} %bitcast.8, f32[32,256]{1,0:T(8,128)} %params_hbm.1, ...), custom_call_target="tpu_custom_call" | custom-call | tf_op jit(solution)/shard_map/analysis/pallas_call | solution.py:586
  56.0 4.0 %finish.1 = (f32[32,512,128]{2,1,0:T(8,128)}, f32[32,256]{1,0:T(8,128)}) custom-call(f32[32,520,128]{2,1,0:T(8,128)S(1)} %get-tuple-element.6.pred_ref, f32[32,256]{1,0:T(8,128)S(1)} %get-tuple-element.7.post_ref), custom_call_target="tpu_custom_call" | custom-call | tf_op jit(solution)/shard_map/finish/pallas_call | solution.py:661

commit v6 on v5

--- a/solution.py
+++ b/solution.py
@@ -14,12 +14,12 @@
 VMEM_BYTES = 67043328
 PARTS = 8
 EARLY = 1
-LATE = 6
+LATE = 8
 FIRST = 1
 BEFORE = 2
-AHEAD = 3
+AHEAD = 4
 MIDDLE = 0
-ADDED = 4
+ADDED = 6
 BACK = 1
 PAD = 8
 WIDE = 256

time: 60.2 us -> 57.8 us (0.960)
  the two profiles are of different devices: /device:TPU:8 before, /device:TPU:0 now
where the time goes in v6:
time: 57.8 us; the launch traced here: 57.6 us
  Pallas kernels  56.3 us (97%)
  between operations  1.29 us (2%)
    pallas_call x1, Pallas kernels, analysis(): pl.pallas_call(functools.partial(analysis_kernel, n_e, n_s), in_specs=[hb...  52.3 us
    pallas_call x1, Pallas kernels, finish(): pl.pallas_call(finish_kernel, in_specs=[vmem, vmem], out_specs=[pl.BlockS...  4.03 us

profile of v6, /device:TPU:0, one launch (start us, length us, event | category | flops | bytes accessed | tf_op | source)
XLA Modules:
  0.0 57.6 jit_solution(12558244514088678987)
XLA Ops:
  1.3 52.3 %analysis.1 = (f32[32,520,128]{2,1,0:T(8,128)S(1)}, f32[32,256]{1,0:T(8,128)S(1)}) custom-call(s32[1024]{0:T(1024)} %pos_hbm.1, s32[1,1]{1,0:T(1,128)} %bitcast.5.count_hbm, s32[1,1024]{1,0:T(1,128)} %bitcast.6, f32[32,1024]{1,0:T(8,128)} %noise_hbm.1, f32[1,1024]{1,0:T(1,128)} %bitcast.7, f32[1,1024]{1,0:T(1,128)} %bitcast.8, f32[32,256]{1,0:T(8,128)} %params_hbm.1, ...), custom_call_target="tpu_custom_call" | custom-call | tf_op jit(solution)/shard_map/analysis/pallas_call | solution.py:586
  53.6 4.0 %finish.1 = (f32[32,512,128]{2,1,0:T(8,128)}, f32[32,256]{1,0:T(8,128)}) custom-call(f32[32,520,128]{2,1,0:T(8,128)S(1)} %get-tuple-element.6.pred_ref, f32[32,256]{1,0:T(8,128)S(1)} %get-tuple-element.7.post_ref), custom_call_target="tpu_custom_call" | custom-call | tf_op jit(solution)/shard_map/finish/pallas_call | solution.py:661
